TPU v7x, 256 devices: a whole 4x4x8 slice. The times are simulated.
256 devices in a mesh: pipe: 2 (over core), slab: 8 (over x, z_hi), dp: 16 (over z_lo, y).
Axes of the slice: x: 4, y: 4, z: 8 (z_hi: 2, z_lo: 4; z = z_hi * 4 + z_lo), core: 2. Of those that a mesh axis runs over, the one named last changes fastest.
Arguments:
- saved_inputs: bfloat16 [2, 2, 16, 2, 16, 16, 512], P('pipe', None, 'dp', None, 'slab'), may hold values from -12 to 12
- loss_cotangent: bfloat16 [2, 16, 2, 16, 16, 512], P(None, 'dp', None, 'slab'), may hold values from -3 to 3
- upstream: bfloat16 [16, 2, 16, 16, 512], P('dp', None, 'slab'), may hold values from -3 to 3
- conv_weight: bfloat16 [2, 512, 13824], P('pipe', 'dp'), may hold values from -0.0546875 to 0.0546875
- adagn_table: bfloat16 [2, 1000, 1024], P('pipe'), may hold values from -3 to 3
- timesteps: int32 [3, 16], P(None, 'dp'), may hold values from 0 to 999
- frame_counts: int32 [3, 16], P(None, 'dp'), may hold values from 1 to 2
Outputs:
- input_grads: bfloat16 [2, 2, 16, 2, 16, 16, 512], P('pipe', None, 'dp', None, 'slab')
- weight_grad: float32 [2, 512, 13824], P('pipe', 'dp')
- embed_grad: float32 [2, 2, 16, 1024], P('pipe', None, 'dp')
All inputs are finite; a program needn't handle non-finite values.
Results may differ from a plain program's by a relative error of at most 0.015.
Values may be sent and summed in bfloat16 or wider, within the bound.
A program may use at most 128 MiB of HBM per device.

v0:
```python
import math

import jax
import jax.numpy as jnp
from jax import lax
from jax.sharding import PartitionSpec as P

GROUPS = 32


EPS = 1e-05


def extended(x, sides, width):
    for axis, dim in sides:
        devices, length = (lax.axis_size(axis), x.shape[dim])
        up = [(i, (i + 1) % devices) for i in range(devices - 1)]
        down = [(j, i) for i, j in up]
        last = lax.slice_in_dim(x, length - width, length, axis=dim)
        initial = lax.slice_in_dim(x, 0, width, axis=dim)
        before = lax.ppermute(last, axis, up)
        after = lax.ppermute(initial, axis, down)
        x = jnp.concatenate([before, x, after], axis=dim)
    return x


def shifted(block, axis, distance):
    devices = range(lax.axis_size(axis))
    route = [(i - distance, i) for i in devices if i - distance in devices]
    return lax.ppermute(block, axis, route)


def group_sums(values, groups):
    summed = jnp.sum(values.reshape(-1, values.shape[-1]), axis=0)
    return jnp.sum(summed.reshape(groups, -1), axis=1)


def silu_grad(preact):
    sigma = jax.nn.sigmoid(preact)
    return sigma * (1.0 + preact * (1.0 - sigma))


def hidden_of(values, mean_c, rstd_c, gain_row, bias_row, mask_now):
    normed = (values - mean_c) * rstd_c
    preact = normed * gain_row + bias_row
    activated = jax.nn.silu(preact) * mask_now[:, None, None, None]
    return (normed, preact, activated)


def norm_terms(moment_one, moment_two, count_now):
    mean_g = moment_one / count_now
    var_g = moment_two / count_now - mean_g * mean_g
    return (mean_g, lax.rsqrt(var_g + EPS))


def tap_stack(padded, frames, slab_rows, cells_wide, mirrored):
    slices = []
    for depth_at in range(3):
        for vertical in range(3):
            for across in range(3):
                if mirrored:
                    offsets = (2 - depth_at, 2 - vertical, 2 - across)
                else:
                    offsets = (depth_at, vertical, across)
                slices.append(
                    padded[
                        ...,
                        offsets[0] : offsets[0] + frames,
                        offsets[1] : offsets[1] + slab_rows,
                        offsets[2] : offsets[2] + cells_wide,
                        :,
                    ]
                )
    return jnp.stack(slices, 0)


def pad_cells(values):
    return jnp.pad(values, ((1, 1), (0, 0), (1, 1), (0, 0)))


def local(
    saved_inputs, loss_cotangent, upstream, conv_weight, adagn_table, timesteps, frame_counts
):
    section_index = lax.axis_index("pipe")
    slab_count = lax.axis_size("slab")
    replicas = lax.axis_size("dp")
    inputs = saved_inputs[0, :, 0]
    tick_count, frames, slab_rows, cells_wide, channels = inputs.shape
    groups = GROUPS
    per_group = channels // groups
    height_total = slab_rows * slab_count
    step_table = adagn_table[0]
    weight_local = conv_weight[0]
    steps_now = lax.dynamic_slice_in_dim(timesteps[:, 0], section_index, tick_count)
    counts_now = lax.dynamic_slice_in_dim(frame_counts[:, 0], section_index, tick_count)
    onehot = (
        steps_now[:, None] == jnp.arange(step_table.shape[0], dtype=jnp.int32)[None, :]
    ).astype(jnp.bfloat16)
    embedded = jnp.dot(onehot, step_table, preferred_element_type=jnp.float32)
    scales = 1.0 + embedded[:, :channels]
    shifts = embedded[:, channels:]
    frame_masks = (jnp.arange(frames, dtype=jnp.int32)[None, :] < counts_now[:, None]).astype(
        jnp.float32
    )
    valid_counts = counts_now.astype(jnp.float32) * float(height_total * cells_wide * per_group)
    weight_norm = 1.0 / math.sqrt(tick_count * replicas * frames * height_total * cells_wide)
    embed_norm = 1.0 / math.sqrt(frames * height_total * cells_wide)
    full_weight = lax.all_gather(weight_local, "dp", axis=0, tiled=True).reshape(
        channels, 27, channels
    )
    dx_list = []
    embed_list = []
    hidden_exts = []
    cotangents = []
    received = None
    for tick_index in range(tick_count):
        values = inputs[tick_index].astype(jnp.float32)
        masked = values * frame_masks[tick_index][:, None, None, None]
        part_one = group_sums(masked, groups)
        part_two = group_sums(masked * values, groups)
        moment_one, moment_two = lax.psum((part_one, part_two), "slab")
        count_now = valid_counts[tick_index]
        mean_g, rstd_g = norm_terms(moment_one, moment_two, count_now)
        mean_c = jnp.repeat(mean_g, per_group)
        rstd_c = jnp.repeat(rstd_g, per_group)
        mask_now = frame_masks[tick_index]
        normed, preact, activated = hidden_of(
            inputs[tick_index].astype(jnp.float32),
            mean_c,
            rstd_c,
            scales[tick_index],
            shifts[tick_index],
            mask_now,
        )
        hidden_ext = extended(activated.astype(jnp.bfloat16), (("slab", 1),), 1)
        hidden_exts.append(hidden_ext)
        incoming = upstream[0] if tick_index == 0 else received
        cotangent = jnp.where(section_index == 1, loss_cotangent[tick_index, 0], incoming)
        cot_rows = extended(cotangent, (("slab", 1),), 1)
        cot_pad = pad_cells(cot_rows)
        tap_slices = tap_stack(cot_pad, frames, slab_rows, cells_wide, True)
        upward = jnp.einsum(
            "tfrwo,oti->frwi", tap_slices, full_weight, preferred_element_type=jnp.float32
        )
        pre_grad = upward * silu_grad(preact) * mask_now[:, None, None, None]
        dnormed = pre_grad * scales[tick_index]
        part_a = group_sums(dnormed, groups)
        part_b = group_sums(dnormed * normed, groups)
        scale_part = jnp.sum(pre_grad * normed, axis=(0, 1, 2))
        shift_part = jnp.sum(pre_grad, axis=(0, 1, 2))
        sum_a, sum_b, scale_sum, shift_sum = lax.psum(
            (part_a, part_b, scale_part, shift_part), "slab"
        )
        branch = (
            rstd_c
            * (
                dnormed
                - jnp.repeat(sum_a / count_now, per_group)
                - normed * jnp.repeat(sum_b / count_now, per_group)
            )
            * mask_now[:, None, None, None]
        )
        result = (cotangent.astype(jnp.float32) + branch).astype(jnp.bfloat16)
        dx_list.append(result)
        embed_list.append(jnp.concatenate([scale_sum, shift_sum]) * embed_norm)
        cotangents.append(cotangent)
        if tick_index + 1 < tick_count:
            received = shifted(result, "pipe", -1)
    cot_all = jnp.stack(cotangents)
    shard_rows = weight_local.shape[0]
    hidden_all = jnp.stack([pad_cells(one_ext) for one_ext in hidden_exts])
    hidden_taps = tap_stack(hidden_all, frames, slab_rows, cells_wide, False)
    grad_term = jnp.einsum(
        "kfrwo,tkfrwi->oti", cot_all, hidden_taps, preferred_element_type=jnp.float32
    )
    grad_shard = lax.psum_scatter(
        (grad_term.reshape(lax.axis_size("dp") * shard_rows, -1) * weight_norm).astype(
            jnp.bfloat16
        ),
        "dp",
        scatter_dimension=0,
        tiled=True,
    ).astype(jnp.float32)
    weight_grad = lax.psum(grad_shard, "slab")
    input_grads = jnp.stack(dx_list)[None, :, None]
    embed_grad = jnp.stack(embed_list)[None, :, None]
    return (input_grads, weight_grad[None], embed_grad)


def solution(mesh):
    placed = (
        P("pipe", None, "dp", None, "slab", None, None),
        P(None, "dp", None, "slab", None, None),
        P("dp", None, "slab", None, None),
        P("pipe", "dp", None),
        P("pipe", None, None),
        P(None, "dp"),
        P(None, "dp"),
    )
    return jax.shard_map(
        local,
        mesh=mesh,
        in_specs=placed,
        out_specs=(
            P("pipe", None, "dp", None, "slab", None, None),
            P("pipe", "dp", None),
            P("pipe", None, "dp", None),
        ),
        check_vma=False,
    )
```

profile of v0, /device:TPU:130, one launch (start us, length us, event | category | flops | bytes accessed | tf_op | source)
XLA Modules:
  0.0 681.5 jit_solution(7426702432679894269)
XLA Ops:
  7.2 0.7 all-gather.3.cloned.1.call-update
  8.0 0.9 bitcast_select_fusion.2
  8.9 1.9 collective-permute-start
  10.8 7.8 %collective-permute-start.1 = (bf16[2,1,16,512]{3,2,1,0:T(8,128)(2,1)S(1)}, bf16[2,1,16,512]{3,2,1,0:T(8,128)(2,1)S(1)}, u32[]{:S(2)}, u32[]{:S(2)}) collective-permute-start(bf16[2,1,16,512]{3,2,1,0:T(8,128)(2,1)S(1)} %get-tuple-element.57), channel_id=1, source_target_pairs={{16,0},{32,16},{48,32},{64,48},{80,64},{96,80},{112,96},{17,1},{33... | collective-permute-start | bytes 98312 | tf_op jit(solution)/shard_map/ppermute | solution.py:22
  18.6 0.7 convert_multiply_fusion.4
  19.4 1.0 fusion.43
  20.8 22.8 %all-reduce.6 = (f32[32]{0:T(128)S(1)}, f32[32]{0:T(128)S(1)}) all-reduce(f32[32]{0:T(128)S(1)} %reduce_sum.183, f32[32]{0:T(128)S(1)} %reduce_sum.181), channel_id=1, replica_groups=mesh['pipe'=2,'slab'=8,'dp'=16] {'slab'}, use_global_device_ids=true, to_apply=%region_5.0 | all-reduce | flops 64 | bytes 512 | tf_op jit(solution)/shard_map/psum | solution.py:121
  43.6 0.7 dynamic-slice_bitcast_fusion
  45.4 0.7 add_rsqrt_fusion.1
  46.9 0.7 constant_dynamic-update-slice_fusion.26
  47.6 0.6 constant_dynamic-update-slice_fusion.25
  48.2 0.6 constant_dynamic-update-slice_fusion.24
  48.8 0.6 constant_dynamic-update-slice_fusion.23
  49.5 0.6 constant_dynamic-update-slice_fusion.22
  50.1 0.6 constant_dynamic-update-slice_fusion.21
  50.8 0.6 constant_dynamic-update-slice_fusion.20
  51.4 0.6 constant_dynamic-update-slice_fusion.19
  52.1 0.6 constant_dynamic-update-slice_fusion.18
  52.7 0.6 constant_dynamic-update-slice_fusion.17
  53.4 0.6 constant_dynamic-update-slice_fusion.16
  54.0 0.6 constant_dynamic-update-slice_fusion.15
  54.6 0.6 constant_dynamic-update-slice_fusion.14
  55.3 0.6 constant_dynamic-update-slice_fusion.13
  55.9 0.6 constant_dynamic-update-slice_fusion.12
  56.6 0.6 constant_dynamic-update-slice_fusion.11
  57.2 0.6 constant_dynamic-update-slice_fusion.10
  57.9 0.6 constant_dynamic-update-slice_fusion.9
  58.5 0.6 constant_dynamic-update-slice_fusion.8
  59.1 0.6 constant_dynamic-update-slice_fusion.7
  59.8 0.6 constant_dynamic-update-slice_fusion.6
  60.4 0.6 constant_dynamic-update-slice_fusion.5
  61.1 0.6 constant_dynamic-update-slice_fusion.4
  61.7 0.6 constant_dynamic-update-slice_fusion.3
  62.4 0.6 constant_dynamic-update-slice_fusion.2
  63.0 0.6 constant_dynamic-update-slice_fusion.1
  63.6 0.6 constant_dynamic-update-slice_fusion
  64.3 105.6 %all-gather.3.cloned.1.call-done = bf16[1,512,13824]{2,1,0:T(8,128)(2,1)} async-done(((bf16[1,32,13824]{2,1,0:T(8,128)(2,1)}), bf16[1,512,13824]{2,1,0:T(8,128)(2,1)}) %all-gather.3.cloned.1.call-update) | async-done | bytes 14155792 | tf_op jit(solution)/shard_map/all_gather | solution.py:108
  169.9 18.7 %copy.101 = bf16[1,512,13824]{1,2,0:T(8,128)(2,1)} copy(bf16[1,512,13824]{2,1,0:T(8,128)(2,1)} %all-gather.3.cloned.1.call-done) | data formatting | bytes 28311552 | tf_op jit(solution)/shard_map/all_gather | solution.py:108
  188.6 10.0 %fusion.42 = (f32[512]{0:T(512)S(1)}, f32[512]{0:T(512)S(1)}, f32[512]{0:T(512)S(1)}, f32[512]{0:T(512)S(1)}, f32[2,2,16,512]{3,2,1,0:T(8,128)S(1)}) fusion(f32[512]{0:T(512)S(1)} %sub.59, f32[512]{0:T(512)S(1)} %mul.241, bf16[1,2,1,2,2,16,512]{6,5,4,3,2,1,0:T(8,128)(2,1)S(1)} %copy-done.3, f32[512]{0:T(512)S(1)} %bitcast.570, ...), kind=kOutput, calls=%fused_computation.194 | convolution fusion | flops 906655744 | bytes 16138248 | tf_op jit(solution)/shard_map/tfrwo,oti->frwi/dot_general | solution.py:142
  199.0 24.9 %all-reduce.5 = (f32[32]{0:T(128)S(1)}, f32[32]{0:T(128)S(1)}, f32[32]{0:T(128)S(1)}, f32[32]{0:T(128)S(1)}) all-reduce(f32[32]{0:T(128)S(1)} %reduce_sum.187, f32[32]{0:T(128)S(1)} %reduce_sum.185, f32[32]{0:T(128)S(1)} %reduce_sum.191, f32[32]{0:T(128)S(1)} %reduce_sum.189), channel_id=1, replica_groups=mesh['pipe'=2,'slab'=8,'dp'=16] {'slab'}, use_global_device_ids=true, to_apply=%region_11.12 | all-reduce | flops 128 | bytes 1024 | tf_op jit(solution)/shard_map/psum | solution.py:151
  223.8 0.6 broadcast_divide_fusion.3
  224.9 1.3 collective-permute-start.2
  226.2 1.8 collective-permute-done.2
  228.1 5.5 collective-permute-start.3
  233.6 4.2 collective-permute-start.4
  237.8 0.7 add_rsqrt_fusion
  238.8 6.4 collective-permute-start.5
  245.2 3.3 collective-permute-start.6
  249.3 9.4 %fusion.6 = f32[2,2,16,512]{3,2,0,1:T(8,128)S(1)} fusion(bf16[512,27,512,1,1]{0,2,3,4,1:T(8,128)(2,1)} %bitcast.562, bf16[27,2,2,16,512]{4,3,2,1,0:T(8,128)(2,1)S(1)} %constant_dynamic-update-slice_fusion.27), kind=kOutput, calls=%fused_computation.63 | convolution fusion | flops 905969664 | bytes 16056320 | tf_op jit(solution)/shard_map/tfrwo,oti->frwi/dot_general | solution.py:142
  258.9 7.3 %collective-permute-start.7 = (bf16[2,1,16,512]{3,2,1,0:T(8,128)(2,1)S(1)}, bf16[2,1,16,512]{3,2,1,0:T(8,128)(2,1)S(1)}, u32[]{:S(2)}, u32[]{:S(2)}) collective-permute-start(bf16[2,1,16,512]{3,2,1,0:T(8,128)(2,1)S(1)} %get-tuple-element.50), channel_id=1, source_target_pairs={{0,16},{16,32},{32,48},{48,64},{64,80},{80,96},{96,112},{1,17},{17... | collective-permute-start | bytes 98312 | tf_op jit(solution)/shard_map/ppermute | solution.py:21
  266.2 3.2 collective-permute-start.8
  269.5 7.5 %collective-permute-done.8 = bf16[2,1,16,512]{3,2,1,0:T(8,128)(2,1)S(1)} collective-permute-done((bf16[2,1,16,512]{3,2,1,0:T(8,128)(2,1)S(1)}, bf16[2,1,16,512]{3,2,1,0:T(8,128)(2,1)S(1)}, u32[]{:S(2)}, u32[]{:S(2)}) %collective-permute-start.8) | collective-permute-done | bytes 32800 | tf_op jit(solution)/shard_map/ppermute | solution.py:22
  278.2 1.7 copy-done.2
  279.9 9.1 %fusion = bf16[512,27,512]{0,2,1:T(8,128)(2,1)} fusion(bf16[27,2,2,2,16,512]{5,4,3,2,1,0:T(8,128)(2,1)} %copy-done.2, bf16[1,2,2,16,512]{4,3,2,1,0:T(8,128)(2,1)S(1)} %bitcast.564, bf16[1,2,2,16,512]{4,3,2,1,0:T(8,128)(2,1)S(1)} %get-tuple-element.46), kind=kOutput, calls=%fused_computation.1 | convolution fusion | flops 1826160640 | bytes 17825792 | tf_op jit(solution)/shard_map/kfrwo,tkfrwi->oti/dot_general | solution.py:173
  289.0 18.6 %copy.108 = bf16[512,13824]{1,0:T(8,128)(2,1)} copy(bf16[512,13824]{0,1:T(8,128)(2,1)} %bitcast.563) | data formatting | bytes 28311552 | tf_op jit(solution)/shard_map/convert_element_type | solution.py:177
  307.7 193.0 %reduce-scatter.2.cloned.1.call-done = bf16[32,13824]{1,0:T(8,128)(2,1)} async-done(((bf16[512,13824]{1,0:T(8,128)(2,1)}), bf16[32,13824]{1,0:T(8,128)(2,1)}) %reduce-scatter.2.cloned.1.call-update) | async-done | bytes 884752 | tf_op jit(solution)/shard_map/reduce_scatter | solution.py:176
  500.7 2.5 bitcast_convert_fusion
  503.6 29.3 %all-reduce.4 = (f32[32]{0:T(128)S(1)}, f32[32]{0:T(128)S(1)}, f32[1,512]{1,0:T(1,128)S(1)}, f32[1,512]{1,0:T(1,128)S(1)}, f32[1,512]{1,0:T(1,128)S(1)}, /*index=5*/f32[1,512]{1,0:T(1,128)S(1)}) all-reduce(f32[32]{0:T(128)S(1)} %reduce_sum.195, f32[32]{0:T(128)S(1)} %reduce_sum.193, ...), channel_id=1, replica_groups=mesh['pipe'=2,'slab'=8,'dp'=16] {'slab'}, use_global_device_ids=true, to_apply=%region_23.24 | all-reduce | flops 2112 | bytes 16896 | tf_op jit(solution)/shard_map/psum | solution.py:151
  533.0 0.6 broadcast_in_dim.47
  533.6 0.6 broadcast_divide_fusion.1
  534.4 0.7 broadcast_divide_fusion
  535.3 0.7 maximum_bitcast_fusion
  536.0 136.1 %all-reduce.9.cloned.1.call-done = f32[1,32,13824]{2,1,0:T(8,128)} async-done(((f32[1,32,13824]{2,1,0:T(8,128)}), f32[1,32,13824]{2,1,0:T(8,128)}) %all-reduce.9.cloned.1.call-update) | async-done | bytes 1769488 | tf_op jit(solution)/shard_map/psum | solution.py:184
  672.1 2.8 copy.209
  (131 shorter events, 6.1 us)
Async XLA Ops:
  7.2 37.8 %copy-start = (bf16[1,1000,1024]{2,1,0:T(8,128)(2,1)S(1)}, bf16[1,1000,1024]{2,1,0:T(8,128)(2,1)}, u32[]{:S(2)}) copy-start(bf16[1,1000,1024]{2,1,0:T(8,128)(2,1)} %param.11) | copy-start | bytes 6144004
  7.2 162.7 %all-gather.3.cloned.1.call-start = ((), (), s32[]{:S(2)}) async-start(), calls=%async_computation.3 | async-start | bytes 15040512 | tf_op jit(solution)/shard_map/all_gather | solution.py:108
  7.9 492.8 %reduce-scatter.2.cloned.1.call-start = ((), (), s32[]{:S(2)}) async-start(), calls=%async_computation.1 | async-start | bytes 15040512 | tf_op jit(solution)/shard_map/reduce_scatter | solution.py:176
  8.9 37.9 %collective-permute-start = (bf16[2,1,16,512]{3,2,1,0:T(8,128)(2,1)S(1)}, bf16[2,1,16,512]{3,2,1,0:T(8,128)(2,1)S(1)}, u32[]{:S(2)}, u32[]{:S(2)}) collective-permute-start(bf16[2,1,16,512]{3,2,1,0:T(8,128)(2,1)S(1)} %get-tuple-element.56), channel_id=1, source_target_pairs={{0,16},{16,32},{32,48},{48,64},{64,80},{80,96},{96,112},{1,17},{17... | collective-permute-start | bytes 98312 | tf_op jit(solution)/shard_map/ppermute | solution.py:21
  10.8 36.0 %collective-permute-start.1 = (bf16[2,1,16,512]{3,2,1,0:T(8,128)(2,1)S(1)}, bf16[2,1,16,512]{3,2,1,0:T(8,128)(2,1)S(1)}, u32[]{:S(2)}, u32[]{:S(2)}) collective-permute-start(bf16[2,1,16,512]{3,2,1,0:T(8,128)(2,1)S(1)} %get-tuple-element.57), channel_id=1, source_target_pairs={{16,0},{32,16},{48,32},{64,48},{80,64},{96,80},{112,96},{17,1},{33... | collective-permute-start | bytes 98312 | tf_op jit(solution)/shard_map/ppermute | solution.py:22
  45.0 10.3 %copy-start.4 = (bf16[2,1,2,2,16,512]{5,4,3,2,1,0:T(8,128)(2,1)S(1)}, bf16[2,1,2,2,16,512]{5,4,3,2,1,0:T(8,128)(2,1)}, u32[]{:S(2)}) copy-start(bf16[2,1,2,2,16,512]{5,4,3,2,1,0:T(8,128)(2,1)} %param.8) | copy-start | bytes 393220
  45.0 10.3 %copy-start.5 = (bf16[1,2,2,16,512]{4,3,2,1,0:T(8,128)(2,1)S(1)}, bf16[1,2,2,16,512]{4,3,2,1,0:T(8,128)(2,1)}, u32[]{:S(2)}) copy-start(bf16[1,2,2,16,512]{4,3,2,1,0:T(8,128)(2,1)} %param.9) | copy-start | bytes 196612
  64.3 124.3 %copy-start.3 = (bf16[1,2,1,2,2,16,512]{6,5,4,3,2,1,0:T(8,128)(2,1)S(1)}, bf16[1,2,1,2,2,16,512]{6,5,4,3,2,1,0:T(8,128)(2,1)}, u32[]{:S(2)}) copy-start(bf16[1,2,1,2,2,16,512]{6,5,4,3,2,1,0:T(8,128)(2,1)} %param.7) | copy-start | bytes 393220
  224.9 3.1 collective-permute-start.2
  228.1 20.5 %collective-permute-start.3 = (bf16[2,1,16,512]{3,2,1,0:T(8,128)(2,1)S(1)}, bf16[2,1,16,512]{3,2,1,0:T(8,128)(2,1)S(1)}, u32[]{:S(2)}, u32[]{:S(2)}) collective-permute-start(bf16[2,1,16,512]{3,2,1,0:T(8,128)(2,1)S(1)} %get-tuple-element.54), channel_id=1, source_target_pairs={{0,16},{16,32},{32,48},{48,64},{64,80},{80,96},{96,112},{1,17},{17... | collective-permute-start | bytes 98312 | tf_op jit(solution)/shard_map/ppermute | solution.py:21
  233.6 15.0 %collective-permute-start.4 = (bf16[2,1,16,512]{3,2,1,0:T(8,128)(2,1)S(1)}, bf16[2,1,16,512]{3,2,1,0:T(8,128)(2,1)S(1)}, u32[]{:S(2)}, u32[]{:S(2)}) collective-permute-start(bf16[2,1,16,512]{3,2,1,0:T(8,128)(2,1)S(1)} %get-tuple-element.55), channel_id=1, source_target_pairs={{16,0},{32,16},{48,32},{64,48},{80,64},{96,80},{112,96},{17,1},{33... | collective-permute-start | bytes 98312 | tf_op jit(solution)/shard_map/ppermute | solution.py:22
  238.8 30.6 %collective-permute-start.5 = (bf16[2,1,16,512]{3,2,1,0:T(8,128)(2,1)S(1)}, bf16[2,1,16,512]{3,2,1,0:T(8,128)(2,1)S(1)}, u32[]{:S(2)}, u32[]{:S(2)}) collective-permute-start(bf16[2,1,16,512]{3,2,1,0:T(8,128)(2,1)S(1)} %get-tuple-element.52), channel_id=1, source_target_pairs={{0,16},{16,32},{32,48},{48,64},{64,80},{80,96},{96,112},{1,17},{17... | collective-permute-start | bytes 98312 | tf_op jit(solution)/shard_map/ppermute | solution.py:21
  245.2 24.2 %collective-permute-start.6 = (bf16[2,1,16,512]{3,2,1,0:T(8,128)(2,1)S(1)}, bf16[2,1,16,512]{3,2,1,0:T(8,128)(2,1)S(1)}, u32[]{:S(2)}, u32[]{:S(2)}) collective-permute-start(bf16[2,1,16,512]{3,2,1,0:T(8,128)(2,1)S(1)} %get-tuple-element.53), channel_id=1, source_target_pairs={{16,0},{32,16},{48,32},{64,48},{80,64},{96,80},{112,96},{17,1},{33... | collective-permute-start | bytes 98312 | tf_op jit(solution)/shard_map/ppermute | solution.py:22
  258.9 10.6 %collective-permute-start.7 = (bf16[2,1,16,512]{3,2,1,0:T(8,128)(2,1)S(1)}, bf16[2,1,16,512]{3,2,1,0:T(8,128)(2,1)S(1)}, u32[]{:S(2)}, u32[]{:S(2)}) collective-permute-start(bf16[2,1,16,512]{3,2,1,0:T(8,128)(2,1)S(1)} %get-tuple-element.50), channel_id=1, source_target_pairs={{0,16},{16,32},{32,48},{48,64},{64,80},{80,96},{96,112},{1,17},{17... | collective-permute-start | bytes 98312 | tf_op jit(solution)/shard_map/ppermute | solution.py:21
  266.2 10.8 %collective-permute-start.8 = (bf16[2,1,16,512]{3,2,1,0:T(8,128)(2,1)S(1)}, bf16[2,1,16,512]{3,2,1,0:T(8,128)(2,1)S(1)}, u32[]{:S(2)}, u32[]{:S(2)}) collective-permute-start(bf16[2,1,16,512]{3,2,1,0:T(8,128)(2,1)S(1)} %get-tuple-element.51), channel_id=1, source_target_pairs={{16,0},{32,16},{48,32},{64,48},{80,64},{96,80},{112,96},{17,1},{33... | collective-permute-start | bytes 98312 | tf_op jit(solution)/shard_map/ppermute | solution.py:22
  278.2 1.7 copy-start.2
  307.7 364.5 %all-reduce.9.cloned.1.call-start = ((), (), s32[]{:S(2)}) async-start(), calls=%async_computation.2 | async-start | bytes 3538944 | tf_op jit(solution)/shard_map/psum | solution.py:184
  535.3 139.6 %copy-start.1 = (bf16[1,1000,1024]{2,1,0:T(8,128)(2,1)S(1)}, bf16[1,1000,1024]{2,1,0:T(8,128)(2,1)}, u32[]{:S(2)}) copy-start(bf16[1,1000,1024]{2,1,0:T(8,128)(2,1)} %param.11) | copy-start | bytes 6144004
Sparse Core Ops, SparseCore 0:
  9.8 160.0 all-gather.2
  307.8 192.8 reduce-scatter.1
  504.0 168.1 all-reduce.8
where the time goes:
time: 688 us; the launch traced here: 681 us
  waiting for transfers between devices  445 us (65%)
  blocking collectives  77 us (11%)
  local copies, waits for them, and re-layouts  61.5 us (9%)
  starting transfers between devices  41.2 us (6%)
  matrix products  28.9 us (4%)
  between operations  14.6 us (2%)
  other arithmetic  13.5 us (2%)
    reduce_scatter x1, waiting for transfers between devices, local(): lax.psum_scatter((grad_term.reshape(lax.axis_size('dp') * shard_rows, -1)...  193 us
    psum x1, waiting for transfers between devices, local(): weight_grad = lax.psum(grad_shard, 'slab')  136 us
    all_gather x1, waiting for transfers between devices, local(): lax.all_gather(weight_local, 'dp', axis=0, tiled=True)  106 us
    psum x2, blocking collectives, local(): lax.psum((part_a, part_b, scale_part, shift_part), 'slab')  54.2 us
    psum x1, blocking collectives, local(): moment_one, moment_two = lax.psum((part_one, part_two), 'slab')  22.8 us
    ppermute x4, starting transfers between devices, extended(): before = lax.ppermute(last, axis, up)  21.2 us
    unnamed x60, local copies, waits for them, and re-layouts  19.8 us
    dot_general x2, matrix products, local(): jnp.einsum('tfrwo,oti->frwi', tap_slices, full_weight, preferred_element_...  19.4 us
  transfers between devices with their start and end apart: 12, of which 5 were waited for; matrix products, arithmetic and copies ran while one was open for 6% of the time, Pallas kernels for 0%

commit v1 on v0

v1 whole, which is shorter than its diff:
```python
import math

import jax
import jax.numpy as jnp
from jax import lax
from jax.sharding import PartitionSpec as P

GROUPS = 32


EPS = 1e-05


def silu_grad(preact):
    sigma = jax.nn.sigmoid(preact)
    return sigma * (1.0 + preact * (1.0 - sigma))


def chunk_group_sums(values, groups_here):
    summed = jnp.sum(values.reshape(-1, values.shape[-1]), axis=0)
    return jnp.sum(summed.reshape(groups_here, -1), axis=1)


def tap_stack(padded, frames, rows, cells_wide):
    slices = []
    for depth_at in range(3):
        for vertical in range(3):
            for across in range(3):
                slices.append(
                    padded[
                        ...,
                        depth_at : depth_at + frames,
                        vertical : vertical + rows,
                        across : across + cells_wide,
                        :,
                    ]
                )
    return jnp.stack(slices, 0)


def local(
    saved_inputs, loss_cotangent, upstream, conv_weight, adagn_table, timesteps, frame_counts
):
    section_index = lax.axis_index("pipe")
    slab_index = lax.axis_index("slab")
    slab_count = lax.axis_size("slab")
    replicas = lax.axis_size("dp")
    inputs = saved_inputs[0, :, 0]
    tick_count, frames, slab_rows, cells_wide, channels = inputs.shape
    height_total = slab_rows * slab_count
    chunk = channels // slab_count
    per_group = channels // GROUPS
    groups_here = chunk // per_group
    step_table = adagn_table[0]
    taps = 27
    weight_local = conv_weight[0].reshape(-1, taps, channels)
    steps_now = lax.dynamic_slice_in_dim(timesteps[:, 0], section_index, tick_count)
    counts_now = lax.dynamic_slice_in_dim(frame_counts[:, 0], section_index, tick_count)
    chunk_start = slab_index * chunk

    weight_cols = lax.dynamic_slice_in_dim(weight_local, chunk_start, chunk, axis=2)
    weight_chunk = lax.all_gather(weight_cols, "dp", axis=0, tiled=True)
    kernel = weight_chunk.reshape(channels, 3, 3, 3, chunk)[:, ::-1, ::-1, ::-1, :]
    kernel = jnp.transpose(kernel, (1, 2, 3, 0, 4))

    inputs_chunk = lax.all_to_all(inputs, "slab", 4, 2, tiled=True)

    weight_norm = 1.0 / math.sqrt(tick_count * replicas * frames * height_total * cells_wide)
    embed_norm = 1.0 / math.sqrt(frames * height_total * cells_wide)

    def full_rows(rows_value):
        return lax.all_gather(rows_value, "slab", axis=1, tiled=True)

    cot_first = jnp.where(section_index == 1, loss_cotangent[0, 0], upstream[0])
    cot_full_first = full_rows(cot_first)
    cot_full_later = full_rows(loss_cotangent[1, 0])

    dx_list = []
    embed_list = []
    hidden_list = []
    cot_list = []
    cot_full = cot_full_first
    for tick_index in range(tick_count):
        steps = steps_now[tick_index]
        count = counts_now[tick_index]
        embedded = lax.dynamic_index_in_dim(step_table, steps, keepdims=False).astype(
            jnp.float32
        )
        gain = 1.0 + lax.dynamic_slice_in_dim(embedded, chunk_start, chunk)
        bias = lax.dynamic_slice_in_dim(embedded, channels + chunk_start, chunk)
        mask = (jnp.arange(frames, dtype=jnp.int32) < count).astype(jnp.float32)
        mask_cells = mask[:, None, None, None]
        valid = count.astype(jnp.float32) * float(height_total * cells_wide * per_group)

        values = inputs_chunk[tick_index].astype(jnp.float32)
        masked = values * mask_cells
        mean_g = chunk_group_sums(masked, groups_here) / valid
        var_g = chunk_group_sums(masked * values, groups_here) / valid - mean_g * mean_g
        rstd_g = lax.rsqrt(var_g + EPS)
        mean_c = jnp.repeat(mean_g, per_group)
        rstd_c = jnp.repeat(rstd_g, per_group)
        normed = (values - mean_c) * rstd_c
        preact = normed * gain + bias
        hidden = (jax.nn.silu(preact) * mask_cells).astype(jnp.bfloat16)
        hidden_list.append(hidden)

        upward = lax.conv_general_dilated(
            cot_full[None],
            kernel,
            window_strides=(1, 1, 1),
            padding=((1, 1), (1, 1), (1, 1)),
            dimension_numbers=("NDHWC", "DHWIO", "NDHWC"),
            preferred_element_type=jnp.float32,
        )[0]
        pre_grad = upward * silu_grad(preact) * mask_cells
        dnormed = pre_grad * gain
        sum_a = chunk_group_sums(dnormed, groups_here) / valid
        sum_b = chunk_group_sums(dnormed * normed, groups_here) / valid
        scale_part = jnp.sum(pre_grad * normed, axis=(0, 1, 2))
        shift_part = jnp.sum(pre_grad, axis=(0, 1, 2))
        branch = (
            rstd_c
            * (dnormed - jnp.repeat(sum_a, per_group) - normed * jnp.repeat(sum_b, per_group))
            * mask_cells
        )
        cot_chunk = lax.dynamic_slice_in_dim(cot_full, chunk_start, chunk, axis=3)
        result = (cot_chunk.astype(jnp.float32) + branch).astype(jnp.bfloat16)
        result_full = lax.all_gather(result, "slab", axis=3, tiled=True)
        dx_list.append(
            lax.dynamic_slice_in_dim(result_full, slab_index * slab_rows, slab_rows, axis=1)
        )
        embed_list.append(jnp.stack([scale_part, shift_part]))
        cot_list.append(cot_full)
        if tick_index + 1 < tick_count:
            received = lax.ppermute(result_full, "pipe", [(1, 0)])
            cot_full = jnp.where(section_index == 1, cot_full_later, received)

    embed_all = lax.all_gather(jnp.stack(embed_list), "slab", axis=2, tiled=True)
    embed_grad = embed_all.reshape(tick_count, 2 * channels) * embed_norm

    cot_all = jnp.stack(cot_list)
    hidden_all = jnp.pad(
        jnp.stack(hidden_list), ((0, 0), (1, 1), (1, 1), (1, 1), (0, 0))
    )
    hidden_taps = tap_stack(hidden_all, frames, height_total, cells_wide)
    grad_term = jnp.einsum(
        "kfrwo,tkfrwi->oti", cot_all, hidden_taps, preferred_element_type=jnp.float32
    )
    grad_shard = lax.psum_scatter(
        (grad_term * weight_norm).astype(jnp.bfloat16),
        "dp",
        scatter_dimension=0,
        tiled=True,
    ).astype(jnp.float32)
    weight_grad = lax.all_gather(grad_shard, "slab", axis=2, tiled=True)
    weight_grad = weight_grad.reshape(weight_grad.shape[0], taps * channels)
    input_grads = jnp.stack(dx_list)[None, :, None]
    return (input_grads, weight_grad[None], embed_grad[None, :, None])


def solution(mesh):
    placed = (
        P("pipe", None, "dp", None, "slab", None, None),
        P(None, "dp", None, "slab", None, None),
        P("dp", None, "slab", None, None),
        P("pipe", "dp", None),
        P("pipe", None, None),
        P(None, "dp"),
        P(None, "dp"),
    )
    return jax.shard_map(
        local,
        mesh=mesh,
        in_specs=placed,
        out_specs=(
            P("pipe", None, "dp", None, "slab", None, None),
            P("pipe", "dp", None),
            P("pipe", None, "dp", None),
        ),
        check_vma=False,
    )
```

time: 688 us -> 774 us (1.12); the launches traced: 681 us -> 759 us
  blocking collectives: 77 us -> 409 us
  waiting for transfers between devices: 445 us -> 259 us
  starting transfers between devices: 41.2 us -> 11.3 us
  local copies, waits for them, and re-layouts: 61.5 us -> 34.1 us
  matrix products: 28.9 us -> 20.9 us
  other arithmetic: 13.5 us -> 5.73 us
    all_gather x0 -> x5, blocking collectives: none -> 409 us  [the longest x2 266 us: local(): result_full = lax.all_gather(result, 'slab', axis=3, tiled=True)]
    psum x1 -> x0, waiting for transfers between devices: 136 us -> none  [local(): weight_grad = lax.psum(grad_shard, 'slab')]
    psum x3 -> x0, blocking collectives: 77 us -> none  [the longest x2 54.2 us: local(): lax.psum((part_a, part_b, scale_part, shift_part), 'slab')]
    ppermute x9 -> x1, starting transfers between devices: 41 us -> 1.29 us  [local(): received = lax.ppermute(result_full, 'pipe', [(1, 0)])]
    reduce_scatter x1, waiting for transfers between devices: 193 us -> 169 us  [local(): lax.psum_scatter((grad_term * weight_norm).astype(jnp.bfloat16), 'dp', sc...]
    dot_general x3 -> x0, matrix products: 19.8 us -> none  [the longest x2 19.4 us: local(): jnp.einsum('tfrwo,oti->frwi', tap_slices, full_weight, preferred_element_...]
    all_gather x1 -> x2, waiting for transfers between devices: 106 us -> 90.2 us  [the longest x1 74.1 us: local(): weight_grad = lax.all_gather(grad_shard, 'slab', axis=2, tiled=True)]
    conv_general_dilated x0 -> x2, matrix products: none -> 15.3 us  [local(): lax.conv_general_dilated(cot_full[None], kernel, window_strides=(1, 1, 1)...]
  transfers between devices with their start and end apart: 12 -> 5, of which waited for: 5 -> 3; matrix products, arithmetic and copies ran while one was open for 6% -> 2% of each run, Pallas kernels for 0% -> 0%
where the time goes in v1:
time: 774 us; the launch traced here: 759 us
  blocking collectives  409 us (53%)
  waiting for transfers between devices  259 us (33%)
  local copies, waits for them, and re-layouts  34.1 us (4%)
  matrix products  20.9 us (3%)
  between operations  19.1 us (2%)
  starting transfers between devices  11.3 us (1%)
    all_gather x2, blocking collectives, local(): result_full = lax.all_gather(result, 'slab', axis=3, tiled=True)  266 us
    reduce_scatter x1, waiting for transfers between devices, local(): lax.psum_scatter((grad_term * weight_norm).astype(jnp.bfloat16), 'dp', sc...  169 us
    all_gather x2, blocking collectives, full_rows(): return lax.all_gather(rows_value, 'slab', axis=1, tiled=True)  92 us
    all_gather x1, waiting for transfers between devices, local(): weight_grad = lax.all_gather(grad_shard, 'slab', axis=2, tiled=True)  74.1 us
    all_gather x1, blocking collectives, local(): lax.all_gather(jnp.stack(embed_list), 'slab', axis=2, tiled=True)  51.5 us
    all_gather x1, waiting for transfers between devices, local(): weight_chunk = lax.all_gather(weight_cols, 'dp', axis=0, tiled=True)  16 us
  transfers between devices with their start and end apart: 5, of which 3 were waited for; matrix products, arithmetic and copies ran while one was open for 2% of the time, Pallas kernels for 0%

profile of v1, /device:TPU:130, one launch (start us, length us, event | category | flops | bytes accessed | tf_op | source)
XLA Modules:
  0.0 759.1 jit_solution(17184056033001340081)
XLA Ops:
  7.3 1.7 reshape_squeeze.3
  8.9 0.1 constant_dynamic-slice_fusion.6
  9.1 0.8 copy.161
  9.9 2.1 copy.156
  12.0 0.7 bitcast_bitcast_fusion
  12.7 1.7 reshape.434
  14.4 9.6 %all-to-all-start = ((bf16[8,2,4096]{2,1,0:T(2,128)(2,1)}), bf16[8,2,4096]{2,1,0:T(2,128)(2,1)S(1)}, u32[]{:S(2)}, u32[]{:S(2)}) async-start(bf16[8,2,4096]{2,1,0:T(2,128)(2,1)} %reshape.434), calls=%async_computation | async-start | bytes 262144 | tf_op jit(solution)/shard_map/all_to_all | solution.py:66
  24.1 0.7 fusion.112
  24.8 0.7 compare_convert_fusion
  25.5 0.6 fusion.111
  26.1 48.4 %all_gather.21 = bf16[2,16,16,512]{3,2,1,0:T(8,128)(2,1)S(1)} all-gather(bf16[2,2,16,512]{3,2,1,0:T(8,128)(2,1)S(1)} %bitcast_select_fusion.1), channel_id=1, replica_groups=mesh['pipe'=2,'slab'=8,'dp'=16] {'slab'}, dimensions={1}, use_global_device_ids=true | all-gather | bytes 589824 | tf_op jit(solution)/shard_map/all_gather | solution.py:72
  74.6 0.6 compare_convert_fusion.1
  78.9 0.3 copy.222
  79.3 0.4 copy.160
  79.8 0.1 slice.148
  81.1 0.8 dynamic-slice_convert_fusion.1
  81.9 0.7 reshape.435
  82.6 1.3 copy.157
  84.0 0.2 fusion.27
  84.3 0.1 reduce_sum.181
  84.5 0.1 reduce_sum.183
  85.0 16.0 %all-gather.4.cloned.1.call-done = bf16[512,27,64]{2,0,1:T(8,128)(2,1)} async-done(((bf16[32,27,64]{2,0,1:T(8,128)(2,1)}), bf16[512,27,64]{2,0,1:T(8,128)(2,1)}) %all-gather.4.cloned.1.call-update) | async-done | bytes 1769488 | tf_op jit(solution)/shard_map/all_gather | solution.py:62
  101.0 7.6 %fusion.20 = f32[2,16,8,3,64]{4,2,3,1,0:T(8,128)S(1)} fusion(bf16[512,3,3,3,64]{4,0,3,2,1:T(8,128)(2,1)} %bitcast.334, bf16[2,16,1,7,2,512]{5,3,4,1,0,2:T(8,128)(2,1)S(1)} %slice.148, bf16[2,16,1,8,3,512]{5,3,4,1,0,2:T(8,128)(2,1)S(1)} %copy.160, pred[8,3]{0,1:T(4,128)(4,1)S(1)} %copy-done.4), kind=kOutput, calls=%fused_computation.44 | convolution fusion | flops 872202240 | bytes 3211288 | tf_op jit(solution)/shard_map/conv_general_dilated | solution.py:107
  108.8 0.2 multiply_reduce_fusion.3
  109.0 0.2 fusion.94
  109.4 0.1 reduce_sum.187
  109.7 0.1 reduce_sum.185
  110.0 0.1 add_convert_fusion.1
  110.2 0.8 copy.165
  111.0 162.6 %all_gather.23 = bf16[2,16,16,512]{2,1,0,3:T(8,128)(2,1)} all-gather(bf16[2,16,16,64]{2,1,0,3:T(8,128)(2,1)S(1)} %copy.165), channel_id=1, replica_groups=mesh['pipe'=2,'slab'=8,'dp'=16] {'slab'}, dimensions={3}, use_global_device_ids=true | all-gather | bytes 589824 | tf_op jit(solution)/shard_map/all_gather | solution.py:128
  273.5 4.4 copy.166
  277.9 1.3 collective-permute-start
  279.3 43.6 %all-gather = bf16[1,1,2,16,16,512]{5,4,3,2,1,0:T(8,128)(2,1)S(1)} all-gather(bf16[1,1,2,2,16,512]{5,4,3,2,1,0:T(8,128)(2,1)S(1)} %slice-done), channel_id=2, replica_groups=mesh['pipe'=2,'slab'=8,'dp'=16] {'slab'}, dimensions={3}, use_global_device_ids=true | all-gather | bytes 589824 | tf_op jit(solution)/shard_map/all_gather | solution.py:72
  323.0 0.1 reduce_sum.189
  323.2 0.1 reduce_sum.191
  323.8 0.3 copy.223
  324.1 0.4 copy.170
  324.6 0.1 slice.151
  324.7 7.6 %fusion.17 = f32[2,16,8,3,64]{4,2,3,1,0:T(8,128)S(1)} fusion(bf16[512,3,3,3,64]{4,0,3,2,1:T(8,128)(2,1)} %bitcast.335, bf16[2,16,1,7,2,512]{5,3,4,1,0,2:T(8,128)(2,1)S(1)} %slice.151, bf16[2,16,1,8,3,512]{5,3,4,1,0,2:T(8,128)(2,1)S(1)} %copy.170, pred[8,3]{0,1:T(4,128)(4,1)S(1)} %copy-done.4), kind=kOutput, calls=%fused_computation.43 | convolution fusion | flops 872202240 | bytes 3211288 | tf_op jit(solution)/shard_map/conv_general_dilated | solution.py:107
  332.5 0.2 fusion.93
  333.4 0.1 fusion.47
  333.7 0.1 fusion.53
  333.9 0.1 fusion.55
  334.0 0.1 fusion.57
  334.9 5.7 fusion
  340.6 0.3 all-gather.6.cloned.1.call-start
  340.9 168.6 %reduce-scatter.2.cloned.1.call-done = bf16[32,27,64]{2,0,1:T(8,128)(2,1)} async-done(((bf16[512,27,64]{2,0,1:T(8,128)(2,1)}), bf16[32,27,64]{2,0,1:T(8,128)(2,1)}) %reduce-scatter.2.cloned.1.call-update) | async-done | bytes 110608 | tf_op jit(solution)/shard_map/reduce_scatter | solution.py:149
  509.5 2.7 copy.209
  512.4 0.1 reduce_sum.195
  512.8 0.1 reduce_sum.193
  513.1 0.2 multiply_reduce_fusion.2
  513.3 0.1 add_convert_fusion
  513.4 0.8 copy.179
  514.2 103.1 %all_gather.25 = bf16[2,16,16,512]{2,1,0,3:T(8,128)(2,1)S(1)} all-gather(bf16[2,16,16,64]{2,1,0,3:T(8,128)(2,1)S(1)} %copy.179), channel_id=1, replica_groups=mesh['pipe'=2,'slab'=8,'dp'=16] {'slab'}, dimensions={3}, use_global_device_ids=true | all-gather | bytes 589824 | tf_op jit(solution)/shard_map/all_gather | solution.py:128
  617.3 0.5 constant_dynamic-slice_fusion
  617.8 0.7 copy.221
  618.5 0.1 copy.211
  618.6 51.5 %all_gather.27 = f32[2,2,512]{1,0,2:T(2,128)S(1)} all-gather(f32[2,2,64]{1,0,2:T(2,128)S(1)} %copy.211), channel_id=1, replica_groups=mesh['pipe'=2,'slab'=8,'dp'=16] {'slab'}, dimensions={2}, use_global_device_ids=true | all-gather | bytes 9216 | tf_op jit(solution)/shard_map/all_gather | solution.py:138
  670.1 0.2 copy.212
  670.3 0.6 mul.507
  671.0 0.7 maximum_bitcast_fusion.1
  671.6 74.1 %all-gather.6.cloned.1.call-done = f32[32,27,512]{1,0,2:T(8,128)} async-done(((f32[32,27,64]{1,0,2:T(8,128)}), f32[32,27,512]{1,0,2:T(8,128)}) %all-gather.6.cloned.1.call-update) | async-done | bytes 1769488 | tf_op jit(solution)/shard_map/all_gather | solution.py:155
  745.8 5.3 copy.210
  751.0 1.6 broadcast_in_dim_reshape.2
  (92 shorter events, 4.8 us)
Async XLA Ops:
  7.2 16.9 %copy-start.2 = (s32[3,1]{0,1:T(1,128)S(1)}, s32[3,1]{0,1:T(1,128)}, u32[]{:S(2)}) copy-start(s32[3,1]{0,1:T(1,128)} %param.12) | copy-start | bytes 40
  7.2 16.9 %copy-start.3 = (s32[3,1]{0,1:T(1,128)S(1)}, s32[3,1]{0,1:T(1,128)}, u32[]{:S(2)}) copy-start(s32[3,1]{0,1:T(1,128)} %param.13) | copy-start | bytes 40
  7.2 18.9 %copy-start.1 = (bf16[1,2,2,16,512]{4,3,2,1,0:T(8,128)(2,1)S(1)}, bf16[1,2,2,16,512]{4,3,2,1,0:T(8,128)(2,1)}, u32[]{:S(2)}) copy-start(bf16[1,2,2,16,512]{4,3,2,1,0:T(8,128)(2,1)} %param.9) | copy-start | bytes 196612
  7.2 18.9 %copy-start = (bf16[2,1,2,2,16,512]{5,4,3,2,1,0:T(8,128)(2,1)S(1)}, bf16[2,1,2,2,16,512]{5,4,3,2,1,0:T(8,128)(2,1)}, u32[]{:S(2)}) copy-start(bf16[2,1,2,2,16,512]{5,4,3,2,1,0:T(8,128)(2,1)} %param.8) | copy-start | bytes 393220
  7.2 93.8 %all-gather.4.cloned.1.call-start = ((), (), s32[]{:S(2)}) async-start(), calls=%async_computation.2 | async-start | bytes 3760128 | tf_op jit(solution)/shard_map/all_gather | solution.py:62
  9.9 91.1 %copy-start.4 = (pred[8,3]{0,1:T(4,128)(4,1)S(1)}, pred[8,3]{0,1:T(4,128)(4,1)}, u32[]{:S(2)}) copy-start(pred[8,3]{0,1:T(4,128)(4,1)} %constant.79) | copy-start | bytes 76
  14.4 67.5 %all-to-all-start = ((bf16[8,2,4096]{2,1,0:T(2,128)(2,1)}), bf16[8,2,4096]{2,1,0:T(2,128)(2,1)S(1)}, u32[]{:S(2)}, u32[]{:S(2)}) async-start(bf16[8,2,4096]{2,1,0:T(2,128)(2,1)} %reshape.434), calls=%async_computation | async-start | bytes 262144 | tf_op jit(solution)/shard_map/all_to_all | solution.py:66
  24.0 485.5 %reduce-scatter.2.cloned.1.call-start = ((), (), s32[]{:S(2)}) async-start(), calls=%async_computation.3 | async-start | bytes 3760128 | tf_op jit(solution)/shard_map/reduce_scatter | solution.py:149
  108.6 170.7 %slice-start = ((bf16[2,1,2,2,16,512]{5,4,3,2,1,0:T(8,128)(2,1)}), bf16[1,1,2,2,16,512]{5,4,3,2,1,0:T(8,128)(2,1)S(1)}, s32[]{:S(2)}) async-start(bf16[2,1,2,2,16,512]{5,4,3,2,1,0:T(8,128)(2,1)} %param.8), calls=%async_computation.5 | async-start | bytes 131072 | tf_op jit(solution)/shard_map/slice | solution.py:76
  277.9 45.7 %collective-permute-start = (bf16[2,16,16,512]{3,2,1,0:T(8,128)(2,1)S(1)}, bf16[2,16,16,512]{3,2,1,0:T(8,128)(2,1)S(1)}, u32[]{:S(2)}, u32[]{:S(2)}) collective-permute-start(bf16[2,16,16,512]{3,2,1,0:T(8,128)(2,1)S(1)} %copy.166), channel_id=1, source_target_pairs={{128,0},{129,1},{130,2},{131,3},{132,4},{133,5},{134,6},{135,7},{1... | collective-permute-start | bytes 1572872 | tf_op jit(solution)/shard_map/ppermute | solution.py:135
  340.6 405.2 %all-gather.6.cloned.1.call-start = ((), (), s32[]{:S(2)}) async-start(), calls=%async_computation.4 | async-start | bytes 9437184 | tf_op jit(solution)/shard_map/all_gather | solution.py:155
Sparse Core Ops, SparseCore 0:
  10.4 90.5 all-gather.3
  340.7 168.7 reduce-scatter.1
  512.7 233.0 all-gather.5

commit v2 on v1

--- a/solution.py
+++ b/solution.py
@@ -19,6 +19,50 @@
 def chunk_group_sums(values, groups_here):
     summed = jnp.sum(values.reshape(-1, values.shape[-1]), axis=0)
     return jnp.sum(summed.reshape(groups_here, -1), axis=1)
+
+
+def shifted_copies(value, axis):
+    devices = lax.axis_size(axis)
+    pieces = [value]
+    for distance in range(1, devices):
+        route = [(i, (i + distance) % devices) for i in range(devices)]
+        pieces.append(lax.ppermute(value, axis, route))
+    return pieces
+
+
+def gather_stack(value, axis):
+    devices = lax.axis_size(axis)
+    here = lax.axis_index(axis)
+    stacked = jnp.stack(shifted_copies(value, axis))
+    order = (here - jnp.arange(devices, dtype=jnp.int32)) % devices
+    return jnp.take(stacked, order, axis=0)
+
+
+def exchange_blocks(blocks, axis):
+    devices = lax.axis_size(axis)
+    here = lax.axis_index(axis)
+    pieces = [lax.dynamic_index_in_dim(blocks, here, keepdims=False)]
+    for distance in range(1, devices):
+        route = [(i, (i + distance) % devices) for i in range(devices)]
+        target = (here + distance) % devices
+        pieces.append(
+            lax.ppermute(lax.dynamic_index_in_dim(blocks, target, keepdims=False), axis, route)
+        )
+    stacked = jnp.stack(pieces)
+    order = (here - jnp.arange(devices, dtype=jnp.int32)) % devices
+    return jnp.take(stacked, order, axis=0)
+
+
+def scatter_sum(blocks, axis):
+    devices = lax.axis_size(axis)
+    here = lax.axis_index(axis)
+    total = lax.dynamic_index_in_dim(blocks, here, keepdims=False).astype(jnp.float32)
+    for distance in range(1, devices):
+        route = [(i, (i + distance) % devices) for i in range(devices)]
+        target = (here + distance) % devices
+        sent = lax.dynamic_index_in_dim(blocks, target, keepdims=False)
+        total = total + lax.ppermute(sent, axis, route).astype(jnp.float32)
+    return total
 
 
 def tap_stack(padded, frames, rows, cells_wide):
@@ -59,21 +103,27 @@
     chunk_start = slab_index * chunk
 
     weight_cols = lax.dynamic_slice_in_dim(weight_local, chunk_start, chunk, axis=2)
-    weight_chunk = lax.all_gather(weight_cols, "dp", axis=0, tiled=True)
+    weight_chunk = gather_stack(weight_cols, "dp")
     kernel = weight_chunk.reshape(channels, 3, 3, 3, chunk)[:, ::-1, ::-1, ::-1, :]
     kernel = jnp.transpose(kernel, (1, 2, 3, 0, 4))
 
-    inputs_chunk = lax.all_to_all(inputs, "slab", 4, 2, tiled=True)
+    outgoing = inputs.reshape(tick_count, frames, slab_rows, cells_wide, slab_count, chunk)
+    outgoing = jnp.transpose(outgoing, (4, 0, 1, 2, 3, 5))
+    incoming = exchange_blocks(outgoing, "slab")
+    inputs_chunk = jnp.transpose(incoming, (1, 2, 0, 3, 4, 5)).reshape(
+        tick_count, frames, height_total, cells_wide, chunk
+    )
 
     weight_norm = 1.0 / math.sqrt(tick_count * replicas * frames * height_total * cells_wide)
     embed_norm = 1.0 / math.sqrt(frames * height_total * cells_wide)
 
-    def full_rows(rows_value):
-        return lax.all_gather(rows_value, "slab", axis=1, tiled=True)
-
     cot_first = jnp.where(section_index == 1, loss_cotangent[0, 0], upstream[0])
-    cot_full_first = full_rows(cot_first)
-    cot_full_later = full_rows(loss_cotangent[1, 0])
+    cot_both = gather_stack(jnp.stack([cot_first, loss_cotangent[1, 0]]), "slab")
+    cot_both = jnp.transpose(cot_both, (1, 2, 0, 3, 4, 5)).reshape(
+        tick_count, frames, height_total, cells_wide, channels
+    )
+    cot_full_first = cot_both[0]
+    cot_full_later = cot_both[1]
 
     dx_list = []
     embed_list = []
@@ -125,17 +175,30 @@
         )
         cot_chunk = lax.dynamic_slice_in_dim(cot_full, chunk_start, chunk, axis=3)
         result = (cot_chunk.astype(jnp.float32) + branch).astype(jnp.bfloat16)
-        result_full = lax.all_gather(result, "slab", axis=3, tiled=True)
-        dx_list.append(
-            lax.dynamic_slice_in_dim(result_full, slab_index * slab_rows, slab_rows, axis=1)
-        )
+        if tick_index + 1 < tick_count:
+            result_full = jnp.transpose(gather_stack(result, "slab"), (1, 2, 3, 0, 4)).reshape(
+                frames, height_total, cells_wide, channels
+            )
+            dx_list.append(
+                lax.dynamic_slice_in_dim(result_full, slab_index * slab_rows, slab_rows, axis=1)
+            )
+        else:
+            outgoing = jnp.transpose(
+                result.reshape(frames, slab_count, slab_rows, cells_wide, chunk), (1, 0, 2, 3, 4)
+            )
+            incoming = exchange_blocks(outgoing, "slab")
+            dx_list.append(
+                jnp.transpose(incoming, (1, 2, 3, 0, 4)).reshape(
+                    frames, slab_rows, cells_wide, channels
+                )
+            )
         embed_list.append(jnp.stack([scale_part, shift_part]))
         cot_list.append(cot_full)
         if tick_index + 1 < tick_count:
             received = lax.ppermute(result_full, "pipe", [(1, 0)])
             cot_full = jnp.where(section_index == 1, cot_full_later, received)
 
-    embed_all = lax.all_gather(jnp.stack(embed_list), "slab", axis=2, tiled=True)
+    embed_all = jnp.transpose(gather_stack(jnp.stack(embed_list), "slab"), (1, 2, 0, 3))
     embed_grad = embed_all.reshape(tick_count, 2 * channels) * embed_norm
 
     cot_all = jnp.stack(cot_list)
@@ -146,13 +209,10 @@
     grad_term = jnp.einsum(
         "kfrwo,tkfrwi->oti", cot_all, hidden_taps, preferred_element_type=jnp.float32
     )
-    grad_shard = lax.psum_scatter(
-        (grad_term * weight_norm).astype(jnp.bfloat16),
-        "dp",
-        scatter_dimension=0,
-        tiled=True,
-    ).astype(jnp.float32)
-    weight_grad = lax.all_gather(grad_shard, "slab", axis=2, tiled=True)
+    terms = (grad_term * weight_norm).astype(jnp.bfloat16)
+    terms = terms.reshape(replicas, channels // replicas, taps, chunk)
+    grad_shard = scatter_sum(terms, "dp")
+    weight_grad = jnp.transpose(gather_stack(grad_shard, "slab"), (1, 2, 0, 3))
     weight_grad = weight_grad.reshape(weight_grad.shape[0], taps * channels)
     input_grads = jnp.stack(dx_list)[None, :, None]
     return (input_grads, weight_grad[None], embed_grad[None, :, None])

time: 774 us -> 526 us (0.68)
  blocking collectives: 409 us -> 0 us
  starting transfers between devices: 11.3 us -> 253 us
  waiting for transfers between devices: 259 us -> 144 us
  local copies, waits for them, and re-layouts: 34.1 us -> 78.6 us
  between operations: 19.1 us -> 7.4 us
  other arithmetic: 5.73 us -> 17.3 us
    all_gather x5 -> x0, blocking collectives: 409 us -> none  [the longest x2 266 us: local(): result_full = lax.all_gather(result, 'slab', axis=3, tiled=True)]
    ppermute x0 -> x72, starting transfers between devices: none -> 251 us  [the longest x43 153 us: shifted_copies(): pieces.append(lax.ppermute(value, axis, route))]
    reduce_scatter x1 -> x0, waiting for transfers between devices: 169 us -> none  [local(): lax.psum_scatter((grad_term * weight_norm).astype(jnp.bfloat16), 'dp', sc...]
    ppermute x0 -> x72, waiting for transfers between devices: none -> 144 us  [the longest x43 92.7 us: shifted_copies(): pieces.append(lax.ppermute(value, axis, route))]
    all_gather x2 -> x0, waiting for transfers between devices: 90.2 us -> none  [the longest x1 74.1 us: local(): weight_grad = lax.all_gather(grad_shard, 'slab', axis=2, tiled=True)]
    unnamed x42 -> x127, local copies, waits for them, and re-layouts: 8.44 us -> 34.2 us
    gather x0 -> x8, local copies, waits for them, and re-layouts: none -> 19.3 us  [the longest x6 16.4 us: gather_stack(): return jnp.take(stacked, order, axis=0)]
    all_gather x3 -> x0, local copies, waits for them, and re-layouts: 9.85 us -> none  [the longest x1 5.25 us: local(): weight_grad = lax.all_gather(grad_shard, 'slab', axis=2, tiled=True)]
  transfers between devices with their start and end apart: 5 -> 73, of which waited for: 3 -> 19; matrix products, arithmetic and copies ran while one was open for 2% -> 14% of each run, Pallas kernels for 0% -> 0%
where the time goes in v2:
time: 526 us; the launch traced here: 516 us
  starting transfers between devices  253 us (48%)
  waiting for transfers between devices  144 us (27%)
  local copies, waits for them, and re-layouts  78.6 us (15%)
  other arithmetic  17.3 us (3%)
  matrix products  15.6 us (3%)
  between operations  7.4 us (1%)
    ppermute x43, starting transfers between devices, shifted_copies(): pieces.append(lax.ppermute(value, axis, route))  153 us
    ppermute x43, waiting for transfers between devices, shifted_copies(): pieces.append(lax.ppermute(value, axis, route))  92.7 us
    ppermute x15, starting transfers between devices, scatter_sum(): total = total + lax.ppermute(sent, axis, route).astype(jnp.float32)  56.6 us
    ppermute x14, starting transfers between devices, exchange_blocks(): lax.ppermute(lax.dynamic_index_in_dim(blocks, target, keepdims=False), ax...  42 us
    unnamed x127, local copies, waits for them, and re-layouts  34.2 us
    ppermute x15, waiting for transfers between devices, scatter_sum(): total = total + lax.ppermute(sent, axis, route).astype(jnp.float32)  32.4 us
    ppermute x14, waiting for transfers between devices, exchange_blocks(): lax.ppermute(lax.dynamic_index_in_dim(blocks, target, keepdims=False), ax...  19.3 us
    gather x6, local copies, waits for them, and re-layouts, gather_stack(): return jnp.take(stacked, order, axis=0)  16.4 us
  transfers between devices with their start and end apart: 73, of which 19 were waited for; matrix products, arithmetic and copies ran while one was open for 14% of the time, Pallas kernels for 0%

profile of v2, /device:TPU:130, one launch (start us, length us, event | category | flops | bytes accessed | tf_op | source)
XLA Modules:
  0.0 516.0 jit_solution(3225038142841121727)
XLA Ops:
  4.9 2.9 collective-permute-start.15
  25.8 2.7 collective-permute-done.8
  28.5 6.0 %collective-permute-start.9 = (bf16[2,2,2,16,64]{4,3,2,1,0:T(8,128)(2,1)S(1)}, bf16[2,2,2,16,64]{4,3,2,1,0:T(8,128)(2,1)S(1)}, u32[]{:S(2)}, u32[]{:S(2)}) collective-permute-start(bf16[2,2,2,16,64]{4,3,2,1,0:T(8,128)(2,1)S(1)} %bitcast.552), channel_id=1, source_target_pairs={{0,48},{16,64},{32,80},{48,96},{64,112},{80,0},{96,16},{112,32},{1... | collective-permute-start | bytes 49160 | tf_op jit(solution)/shard_map/ppermute | solution.py:49
  34.6 2.7 collective-permute-done.9
  38.4 4.3 collective-permute-done.10
  42.7 7.3 %collective-permute-start.11 = (bf16[2,2,2,16,64]{4,3,2,1,0:T(8,128)(2,1)S(1)}, bf16[2,2,2,16,64]{4,3,2,1,0:T(8,128)(2,1)S(1)}, u32[]{:S(2)}, u32[]{:S(2)}) collective-permute-start(bf16[2,2,2,16,64]{4,3,2,1,0:T(8,128)(2,1)S(1)} %bitcast.550), channel_id=1, source_target_pairs={{0,80},{16,96},{32,112},{48,0},{64,16},{80,32},{96,48},{112,64},{1... | collective-permute-start | bytes 49160 | tf_op jit(solution)/shard_map/ppermute | solution.py:49
  49.9 3.0 collective-permute-done.11
  52.9 3.2 collective-permute-start.12
  57.7 4.0 collective-permute-start.13
  61.7 5.1 collective-permute-done.13
  66.8 2.1 collective-permute-start.18
  71.3 14.4 %collective-permute-start.19 = (bf16[32,27,64]{2,1,0:T(8,128)(2,1)}, bf16[32,27,64]{2,1,0:T(8,128)(2,1)S(1)}, u32[]{:S(2)}, u32[]{:S(2)}) collective-permute-start(bf16[32,27,64]{2,1,0:T(8,128)(2,1)} %get-tuple-element.34), channel_id=1, source_target_pairs={{0,6},{1,7},{2,8},{3,9},{4,10},{5,11},{6,12},{7,13},{8,14},{9,15},... | collective-permute-start | bytes 331784 | tf_op jit(solution)/shard_map/ppermute | solution.py:29
  91.3 3.8 collective-permute-start.22
  95.9 9.5 %collective-permute-done.18 = bf16[32,27,64]{2,1,0:T(8,128)(2,1)S(1)} collective-permute-done((bf16[32,27,64]{2,1,0:T(8,128)(2,1)}, bf16[32,27,64]{2,1,0:T(8,128)(2,1)S(1)}, u32[]{:S(2)}, u32[]{:S(2)}) %collective-permute-start.18) | collective-permute-done | bytes 110624 | tf_op jit(solution)/shard_map/ppermute | solution.py:29
  106.1 5.1 collective-permute-done.19
  111.2 4.0 collective-permute-start.24
  115.9 15.7 %collective-permute-start.25 = (bf16[32,27,64]{2,1,0:T(8,128)(2,1)}, bf16[32,27,64]{2,1,0:T(8,128)(2,1)S(1)}, u32[]{:S(2)}, u32[]{:S(2)}) collective-permute-start(bf16[32,27,64]{2,1,0:T(8,128)(2,1)} %get-tuple-element.34), channel_id=1, source_target_pairs={{0,12},{1,13},{2,14},{3,15},{4,0},{5,1},{6,2},{7,3},{8,4},{9,5},{1... | collective-permute-start | bytes 331784 | tf_op jit(solution)/shard_map/ppermute | solution.py:29
  133.7 22.0 %collective-permute-start.27 = (bf16[32,27,64]{2,1,0:T(8,128)(2,1)}, bf16[32,27,64]{2,1,0:T(8,128)(2,1)S(1)}, u32[]{:S(2)}, u32[]{:S(2)}) collective-permute-start(bf16[32,27,64]{2,1,0:T(8,128)(2,1)} %get-tuple-element.34), channel_id=1, source_target_pairs={{0,14},{1,15},{2,0},{3,1},{4,2},{5,3},{6,4},{7,5},{8,6},{9,7},{10,... | collective-permute-start | bytes 331784 | tf_op jit(solution)/shard_map/ppermute | solution.py:29
  156.5 5.5 %collective-permute-start.28 = (bf16[32,27,64]{2,1,0:T(8,128)(2,1)}, bf16[32,27,64]{2,1,0:T(8,128)(2,1)S(1)}, u32[]{:S(2)}, u32[]{:S(2)}) collective-permute-start(bf16[32,27,64]{2,1,0:T(8,128)(2,1)} %get-tuple-element.34), channel_id=1, source_target_pairs={{0,15},{1,0},{2,1},{3,2},{4,3},{5,4},{6,5},{7,6},{8,7},{9,8},{10,9... | collective-permute-start | bytes 331784 | tf_op jit(solution)/shard_map/ppermute | solution.py:29
  162.7 3.0 collective-permute-start
  166.5 4.6 collective-permute-start.1
  171.8 2.9 collective-permute-start.2
  176.3 4.0 collective-permute-start.4
  181.0 5.4 %gather_fusion.2 = bf16[16,32,27,64]{3,2,1,0:T(8,128)(2,1)} fusion(bf16[16,32,27,64]{3,2,1,0:T(8,128)(2,1)} %bitcast_dynamic-update-slice_fusion.9, s32[1024]{0:T(1024)} %pad_clamp_fusion), kind=kCustom, calls=%fused_computation.2 | custom fusion | bytes 3539008 | tf_op jit(solution)/shard_map/jit(_take)/gather | solution.py:38
  186.4 5.4 %copy.56 = bf16[16,32,27,64]{3,1,0,2:T(8,128)(2,1)} copy(bf16[16,32,27,64]{3,2,1,0:T(8,128)(2,1)} %gather_fusion.2) | data formatting | bytes 3538944 | tf_op jit(solution)/shard_map/jit(_take)/gather | solution.py:38
  191.8 2.7 collective-permute-start.5
  194.5 5.0 collective-permute-start.6
  199.6 6.5 %collective-permute-done.6 = bf16[2,2,2,16,512]{4,3,2,1,0:T(8,128)(2,1)S(1)} collective-permute-done((bf16[2,2,2,16,512]{4,3,2,1,0:T(8,128)(2,1)S(1)}, bf16[2,2,2,16,512]{4,3,2,1,0:T(8,128)(2,1)S(1)}, u32[]{:S(2)}, u32[]{:S(2)}) %collective-permute-start.6) | collective-permute-done | bytes 131104 | tf_op jit(solution)/shard_map/ppermute | solution.py:29
  209.0 5.7 %fusion.17 = f32[2,16,8,3,64]{4,2,3,1,0:T(8,128)S(1)} fusion(bf16[512,3,3,3,64]{4,0,3,2,1:T(8,128)(2,1)S(1)} %bitcast.533, pred[512]{0:T(512)(128)(4,1)S(1)} %copy-done.18, bf16[2,16,1,7,2,512]{5,3,4,1,0,2:T(8,128)(2,1)S(1)} %slice.176, bf16[2,16,1,8,3,512]{5,3,4,1,0,2:T(8,128)(2,1)S(1)} %copy.55, pred[8,3]{0,1:T(4,128)(4,1)S(1)} %copy-done.19), kind=kOutput, calls=%fused_computation.52 | convolution fusion | flops 873086976 | bytes 3211800 | tf_op jit(solution)/shard_map/conv_general_dilated | solution.py:157
  220.1 6.9 %collective-permute-start.31 = (bf16[2,16,16,64]{3,2,1,0:T(8,128)(2,1)S(1)}, bf16[2,16,16,64]{3,2,1,0:T(8,128)(2,1)S(1)}, u32[]{:S(2)}, u32[]{:S(2)}) collective-permute-start(bf16[2,16,16,64]{3,2,1,0:T(8,128)(2,1)S(1)} %get-tuple-element.30), channel_id=1, source_target_pairs={{0,48},{16,64},{32,80},{48,96},{64,112},{80,0},{96,16},{112,32},{1... | collective-permute-start | bytes 196616 | tf_op jit(solution)/shard_map/ppermute | solution.py:29
  227.9 4.2 collective-permute-start.33
  232.7 4.3 collective-permute-start.35
  237.1 2.2 collective-permute-done.33
  239.3 3.2 collective-permute-done.35
  250.8 6.4 %fusion.20 = f32[2,16,8,3,64]{4,2,3,1,0:T(8,128)S(1)} fusion(bf16[512,3,3,3,64]{4,0,3,2,1:T(8,128)(2,1)S(1)} %bitcast.534, pred[512]{0:T(512)(128)(4,1)} %broadcast_in_dim.120, bf16[2,16,1,7,2,512]{5,3,4,1,0,2:T(8,128)(2,1)S(1)} %slice.180, bf16[2,16,1,8,3,512]{5,3,4,1,0,2:T(8,128)(2,1)S(1)} %copy.65, pred[8,3]{0,1:T(4,128)(4,1)} %constant.407), kind=kOutput, calls=%fused_computation.53 | convolution fusion | flops 873086976 | bytes 3211800 | tf_op jit(solution)/shard_map/conv_general_dilated | solution.py:157
  260.6 3.9 collective-permute-start.66
  265.3 3.7 collective-permute-start.68
  269.0 2.4 collective-permute-start.69
  271.4 3.6 collective-permute-start.70
  277.3 3.5 fusion
  280.8 3.4 copy.106
  289.1 3.8 collective-permute-start.72
  294.1 3.1 collective-permute-start.37
  298.7 5.0 collective-permute-start.39
  305.6 3.6 collective-permute-start.41
  315.9 2.8 collective-permute-start.43
  320.1 11.2 %collective-permute-start.58 = (bf16[32,27,64]{2,0,1:T(8,128)(2,1)}, bf16[32,27,64]{2,0,1:T(8,128)(2,1)}, u32[]{:S(2)}, u32[]{:S(2)}) collective-permute-start(bf16[32,27,64]{2,0,1:T(8,128)(2,1)} %get-tuple-element.36), channel_id=1, source_target_pairs={{0,15},{1,0},{2,1},{3,2},{4,3},{5,4},{6,5},{7,6},{8,7},{9,8},{10,9... | collective-permute-start | bytes 331784 | tf_op jit(solution)/shard_map/ppermute | solution.py:64
  337.5 5.2 %collective-permute-start.53 = (bf16[32,27,64]{2,0,1:T(8,128)(2,1)}, bf16[32,27,64]{2,0,1:T(8,128)(2,1)}, u32[]{:S(2)}, u32[]{:S(2)}) collective-permute-start(bf16[32,27,64]{2,0,1:T(8,128)(2,1)} %get-tuple-element.41), channel_id=1, source_target_pairs={{0,10},{1,11},{2,12},{3,13},{4,14},{5,15},{6,0},{7,1},{8,2},{9,3},... | collective-permute-start | bytes 331784 | tf_op jit(solution)/shard_map/ppermute | solution.py:64
  342.7 4.2 collective-permute-done.56
  347.0 24.6 %collective-permute-start.51 = (bf16[32,27,64]{2,0,1:T(8,128)(2,1)}, bf16[32,27,64]{2,0,1:T(8,128)(2,1)}, u32[]{:S(2)}, u32[]{:S(2)}) collective-permute-start(bf16[32,27,64]{2,0,1:T(8,128)(2,1)} %get-tuple-element.43), channel_id=1, source_target_pairs={{0,8},{1,9},{2,10},{3,11},{4,12},{5,13},{6,14},{7,15},{8,0},{9,1},... | collective-permute-start | bytes 331784 | tf_op jit(solution)/shard_map/ppermute | solution.py:64
  371.6 7.1 %collective-permute-start.49 = (bf16[32,27,64]{2,0,1:T(8,128)(2,1)}, bf16[32,27,64]{2,0,1:T(8,128)(2,1)}, u32[]{:S(2)}, u32[]{:S(2)}) collective-permute-start(bf16[32,27,64]{2,0,1:T(8,128)(2,1)} %get-tuple-element.45), channel_id=1, source_target_pairs={{0,6},{1,7},{2,8},{3,9},{4,10},{5,11},{6,12},{7,13},{8,14},{9,15},... | collective-permute-start | bytes 331784 | tf_op jit(solution)/shard_map/ppermute | solution.py:64
  379.3 7.8 %collective-permute-start.47 = (bf16[32,27,64]{2,0,1:T(8,128)(2,1)}, bf16[32,27,64]{2,0,1:T(8,128)(2,1)}, u32[]{:S(2)}, u32[]{:S(2)}) collective-permute-start(bf16[32,27,64]{2,0,1:T(8,128)(2,1)} %get-tuple-element.47), channel_id=1, source_target_pairs={{0,4},{1,5},{2,6},{3,7},{4,8},{5,9},{6,10},{7,11},{8,12},{9,13},{1... | collective-permute-start | bytes 331784 | tf_op jit(solution)/shard_map/ppermute | solution.py:64
  387.1 14.4 %collective-permute-done.51 = bf16[32,27,64]{2,0,1:T(8,128)(2,1)} collective-permute-done((bf16[32,27,64]{2,0,1:T(8,128)(2,1)}, bf16[32,27,64]{2,0,1:T(8,128)(2,1)}, u32[]{:S(2)}, u32[]{:S(2)}) %collective-permute-start.51) | collective-permute-done | bytes 110624 | tf_op jit(solution)/shard_map/ppermute | solution.py:64
  402.5 2.2 gather_fusion.4
  404.8 11.8 %collective-permute-done.48 = bf16[32,27,64]{2,0,1:T(8,128)(2,1)} collective-permute-done((bf16[32,27,64]{2,0,1:T(8,128)(2,1)}, bf16[32,27,64]{2,0,1:T(8,128)(2,1)}, u32[]{:S(2)}, u32[]{:S(2)}) %collective-permute-start.48) | collective-permute-done | bytes 110624 | tf_op jit(solution)/shard_map/ppermute | solution.py:64
  416.6 3.4 bitcast_dynamic-update-slice_fusion.7
  423.4 7.8 %collective-permute-start.61 = (f32[32,27,64]{2,0,1:T(8,128)}, f32[32,27,64]{2,0,1:T(8,128)S(1)}, u32[]{:S(2)}, u32[]{:S(2)}) collective-permute-start(f32[32,27,64]{2,0,1:T(8,128)} %get-tuple-element.26), channel_id=1, source_target_pairs={{0,48},{16,64},{32,80},{48,96},{64,112},{80,0},{96,16},{112,32},{1... | collective-permute-start | bytes 663560 | tf_op jit(solution)/shard_map/ppermute | solution.py:29
  433.5 2.6 collective-permute-done.59
  436.2 3.0 collective-permute-start.64
  440.1 14.4 %collective-permute-done.60 = f32[32,27,64]{2,0,1:T(8,128)S(1)} collective-permute-done((f32[32,27,64]{2,0,1:T(8,128)}, f32[32,27,64]{2,0,1:T(8,128)S(1)}, u32[]{:S(2)}, u32[]{:S(2)}) %collective-permute-start.60) | collective-permute-done | bytes 221216 | tf_op jit(solution)/shard_map/ppermute | solution.py:29
  456.8 8.1 %collective-permute-done.63 = f32[32,27,64]{2,0,1:T(8,128)S(1)} collective-permute-done((f32[32,27,64]{2,0,1:T(8,128)}, f32[32,27,64]{2,0,1:T(8,128)S(1)}, u32[]{:S(2)}, u32[]{:S(2)}) %collective-permute-start.63) | collective-permute-done | bytes 221216 | tf_op jit(solution)/shard_map/ppermute | solution.py:29
  466.5 40.9 %collective-permute-done.65 = f32[32,27,64]{2,0,1:T(8,128)S(1)} collective-permute-done((f32[32,27,64]{2,0,1:T(8,128)}, f32[32,27,64]{2,0,1:T(8,128)S(1)}, u32[]{:S(2)}, u32[]{:S(2)}) %collective-permute-start.65) | collective-permute-done | bytes 221216 | tf_op jit(solution)/shard_map/ppermute | solution.py:29
  508.3 2.9 gather_fusion.5
  511.7 2.1 copy.107
  (341 shorter events, 100.1 us)
Async XLA Ops:
  3.3 68.0 %collective-permute-start.14 = (bf16[32,27,64]{2,1,0:T(8,128)(2,1)}, bf16[32,27,64]{2,1,0:T(8,128)(2,1)}, u32[]{:S(2)}, u32[]{:S(2)}) collective-permute-start(bf16[32,27,64]{2,1,0:T(8,128)(2,1)} %get-tuple-element.34), channel_id=1, source_target_pairs={{0,1},{1,2},{2,3},{3,4},{4,5},{5,6},{6,7},{7,8},{8,9},{9,10},{10,1... | collective-permute-start | bytes 331784 | tf_op jit(solution)/shard_map/ppermute | solution.py:29
  4.9 82.5 %collective-permute-start.15 = (bf16[32,27,64]{2,1,0:T(8,128)(2,1)}, bf16[32,27,64]{2,1,0:T(8,128)(2,1)}, u32[]{:S(2)}, u32[]{:S(2)}) collective-permute-start(bf16[32,27,64]{2,1,0:T(8,128)(2,1)} %get-tuple-element.34), channel_id=1, source_target_pairs={{0,2},{1,3},{2,4},{3,5},{4,6},{5,7},{6,8},{7,9},{8,10},{9,11},{10,... | collective-permute-start | bytes 331784 | tf_op jit(solution)/shard_map/ppermute | solution.py:29
  7.8 81.2 %collective-permute-start.16 = (bf16[32,27,64]{2,1,0:T(8,128)(2,1)}, bf16[32,27,64]{2,1,0:T(8,128)(2,1)S(1)}, u32[]{:S(2)}, u32[]{:S(2)}) collective-permute-start(bf16[32,27,64]{2,1,0:T(8,128)(2,1)} %get-tuple-element.34), channel_id=1, source_target_pairs={{0,3},{1,4},{2,5},{3,6},{4,7},{5,8},{6,9},{7,10},{8,11},{9,12},{10... | collective-permute-start | bytes 331784 | tf_op jit(solution)/shard_map/ppermute | solution.py:29
  9.6 81.7 %collective-permute-start.17 = (bf16[32,27,64]{2,1,0:T(8,128)(2,1)}, bf16[32,27,64]{2,1,0:T(8,128)(2,1)S(1)}, u32[]{:S(2)}, u32[]{:S(2)}) collective-permute-start(bf16[32,27,64]{2,1,0:T(8,128)(2,1)} %get-tuple-element.34), channel_id=1, source_target_pairs={{0,4},{1,5},{2,6},{3,7},{4,8},{5,9},{6,10},{7,11},{8,12},{9,13},{1... | collective-permute-start | bytes 331784 | tf_op jit(solution)/shard_map/ppermute | solution.py:29
  12.4 12.2 %collective-permute-start.7 = (bf16[2,2,2,16,64]{4,3,2,1,0:T(8,128)(2,1)S(1)}, bf16[2,2,2,16,64]{4,3,2,1,0:T(8,128)(2,1)S(1)}, u32[]{:S(2)}, u32[]{:S(2)}) collective-permute-start(bf16[2,2,2,16,64]{4,3,2,1,0:T(8,128)(2,1)S(1)} %bitcast.547), channel_id=1, source_target_pairs={{0,16},{16,32},{32,48},{48,64},{64,80},{80,96},{96,112},{112,0},{1... | collective-permute-start | bytes 49160 | tf_op jit(solution)/shard_map/ppermute | solution.py:49
  42.7 10.2 %collective-permute-start.11 = (bf16[2,2,2,16,64]{4,3,2,1,0:T(8,128)(2,1)S(1)}, bf16[2,2,2,16,64]{4,3,2,1,0:T(8,128)(2,1)S(1)}, u32[]{:S(2)}, u32[]{:S(2)}) collective-permute-start(bf16[2,2,2,16,64]{4,3,2,1,0:T(8,128)(2,1)S(1)} %bitcast.550), channel_id=1, source_target_pairs={{0,80},{16,96},{32,112},{48,0},{64,16},{80,32},{96,48},{112,64},{1... | collective-permute-start | bytes 49160 | tf_op jit(solution)/shard_map/ppermute | solution.py:49
  66.8 38.6 %collective-permute-start.18 = (bf16[32,27,64]{2,1,0:T(8,128)(2,1)}, bf16[32,27,64]{2,1,0:T(8,128)(2,1)S(1)}, u32[]{:S(2)}, u32[]{:S(2)}) collective-permute-start(bf16[32,27,64]{2,1,0:T(8,128)(2,1)} %get-tuple-element.34), channel_id=1, source_target_pairs={{0,5},{1,6},{2,7},{3,8},{4,9},{5,10},{6,11},{7,12},{8,13},{9,14},{... | collective-permute-start | bytes 331784 | tf_op jit(solution)/shard_map/ppermute | solution.py:29
  71.3 39.9 %collective-permute-start.19 = (bf16[32,27,64]{2,1,0:T(8,128)(2,1)}, bf16[32,27,64]{2,1,0:T(8,128)(2,1)S(1)}, u32[]{:S(2)}, u32[]{:S(2)}) collective-permute-start(bf16[32,27,64]{2,1,0:T(8,128)(2,1)} %get-tuple-element.34), channel_id=1, source_target_pairs={{0,6},{1,7},{2,8},{3,9},{4,10},{5,11},{6,12},{7,13},{8,14},{9,15},... | collective-permute-start | bytes 331784 | tf_op jit(solution)/shard_map/ppermute | solution.py:29
  87.3 28.5 %collective-permute-start.20 = (bf16[32,27,64]{2,1,0:T(8,128)(2,1)}, bf16[32,27,64]{2,1,0:T(8,128)(2,1)S(1)}, u32[]{:S(2)}, u32[]{:S(2)}) collective-permute-start(bf16[32,27,64]{2,1,0:T(8,128)(2,1)} %get-tuple-element.34), channel_id=1, source_target_pairs={{0,7},{1,8},{2,9},{3,10},{4,11},{5,12},{6,13},{7,14},{8,15},{9,0},... | collective-permute-start | bytes 331784 | tf_op jit(solution)/shard_map/ppermute | solution.py:29
  89.0 43.3 %collective-permute-start.21 = (bf16[32,27,64]{2,1,0:T(8,128)(2,1)}, bf16[32,27,64]{2,1,0:T(8,128)(2,1)S(1)}, u32[]{:S(2)}, u32[]{:S(2)}) collective-permute-start(bf16[32,27,64]{2,1,0:T(8,128)(2,1)} %get-tuple-element.34), channel_id=1, source_target_pairs={{0,8},{1,9},{2,10},{3,11},{4,12},{5,13},{6,14},{7,15},{8,0},{9,1},... | collective-permute-start | bytes 331784 | tf_op jit(solution)/shard_map/ppermute | solution.py:29
  91.3 42.4 %collective-permute-start.22 = (bf16[32,27,64]{2,1,0:T(8,128)(2,1)}, bf16[32,27,64]{2,1,0:T(8,128)(2,1)S(1)}, u32[]{:S(2)}, u32[]{:S(2)}) collective-permute-start(bf16[32,27,64]{2,1,0:T(8,128)(2,1)} %get-tuple-element.34), channel_id=1, source_target_pairs={{0,9},{1,10},{2,11},{3,12},{4,13},{5,14},{6,15},{7,0},{8,1},{9,2},... | collective-permute-start | bytes 331784 | tf_op jit(solution)/shard_map/ppermute | solution.py:29
  105.4 51.1 %collective-permute-start.23 = (bf16[32,27,64]{2,1,0:T(8,128)(2,1)}, bf16[32,27,64]{2,1,0:T(8,128)(2,1)S(1)}, u32[]{:S(2)}, u32[]{:S(2)}) collective-permute-start(bf16[32,27,64]{2,1,0:T(8,128)(2,1)} %get-tuple-element.34), channel_id=1, source_target_pairs={{0,10},{1,11},{2,12},{3,13},{4,14},{5,15},{6,0},{7,1},{8,2},{9,3},... | collective-permute-start | bytes 331784 | tf_op jit(solution)/shard_map/ppermute | solution.py:29
  111.2 51.6 %collective-permute-start.24 = (bf16[32,27,64]{2,1,0:T(8,128)(2,1)}, bf16[32,27,64]{2,1,0:T(8,128)(2,1)S(1)}, u32[]{:S(2)}, u32[]{:S(2)}) collective-permute-start(bf16[32,27,64]{2,1,0:T(8,128)(2,1)} %get-tuple-element.34), channel_id=1, source_target_pairs={{0,11},{1,12},{2,13},{3,14},{4,15},{5,0},{6,1},{7,2},{8,3},{9,4},{... | collective-permute-start | bytes 331784 | tf_op jit(solution)/shard_map/ppermute | solution.py:29
  115.9 50.6 %collective-permute-start.25 = (bf16[32,27,64]{2,1,0:T(8,128)(2,1)}, bf16[32,27,64]{2,1,0:T(8,128)(2,1)S(1)}, u32[]{:S(2)}, u32[]{:S(2)}) collective-permute-start(bf16[32,27,64]{2,1,0:T(8,128)(2,1)} %get-tuple-element.34), channel_id=1, source_target_pairs={{0,12},{1,13},{2,14},{3,15},{4,0},{5,1},{6,2},{7,3},{8,4},{9,5},{1... | collective-permute-start | bytes 331784 | tf_op jit(solution)/shard_map/ppermute | solution.py:29
  132.3 39.5 %collective-permute-start.26 = (bf16[32,27,64]{2,1,0:T(8,128)(2,1)}, bf16[32,27,64]{2,1,0:T(8,128)(2,1)S(1)}, u32[]{:S(2)}, u32[]{:S(2)}) collective-permute-start(bf16[32,27,64]{2,1,0:T(8,128)(2,1)} %get-tuple-element.34), channel_id=1, source_target_pairs={{0,13},{1,14},{2,15},{3,0},{4,1},{5,2},{6,3},{7,4},{8,5},{9,6},{10... | collective-permute-start | bytes 331784 | tf_op jit(solution)/shard_map/ppermute | solution.py:29
  133.7 41.7 %collective-permute-start.27 = (bf16[32,27,64]{2,1,0:T(8,128)(2,1)}, bf16[32,27,64]{2,1,0:T(8,128)(2,1)S(1)}, u32[]{:S(2)}, u32[]{:S(2)}) collective-permute-start(bf16[32,27,64]{2,1,0:T(8,128)(2,1)} %get-tuple-element.34), channel_id=1, source_target_pairs={{0,14},{1,15},{2,0},{3,1},{4,2},{5,3},{6,4},{7,5},{8,6},{9,7},{10,... | collective-permute-start | bytes 331784 | tf_op jit(solution)/shard_map/ppermute | solution.py:29
  156.5 19.8 %collective-permute-start.28 = (bf16[32,27,64]{2,1,0:T(8,128)(2,1)}, bf16[32,27,64]{2,1,0:T(8,128)(2,1)S(1)}, u32[]{:S(2)}, u32[]{:S(2)}) collective-permute-start(bf16[32,27,64]{2,1,0:T(8,128)(2,1)} %get-tuple-element.34), channel_id=1, source_target_pairs={{0,15},{1,0},{2,1},{3,2},{4,3},{5,4},{6,5},{7,6},{8,7},{9,8},{10,9... | collective-permute-start | bytes 331784 | tf_op jit(solution)/shard_map/ppermute | solution.py:29
  162.7 29.1 %collective-permute-start = (bf16[2,2,2,16,512]{4,3,2,1,0:T(8,128)(2,1)S(1)}, bf16[2,2,2,16,512]{4,3,2,1,0:T(8,128)(2,1)S(1)}, u32[]{:S(2)}, u32[]{:S(2)}) collective-permute-start(bf16[2,2,2,16,512]{4,3,2,1,0:T(8,128)(2,1)S(1)} %pad_maximum_fusion.1), channel_id=1, source_target_pairs={{0,16},{16,32},{32,48},{48,64},{64,80},{80,96},{96,112},{112,0},{1... | collective-permute-start | bytes 393224 | tf_op jit(solution)/shard_map/ppermute | solution.py:29
  166.5 28.0 %collective-permute-start.1 = (bf16[2,2,2,16,512]{4,3,2,1,0:T(8,128)(2,1)S(1)}, bf16[2,2,2,16,512]{4,3,2,1,0:T(8,128)(2,1)S(1)}, u32[]{:S(2)}, u32[]{:S(2)}) collective-permute-start(bf16[2,2,2,16,512]{4,3,2,1,0:T(8,128)(2,1)S(1)} %pad_maximum_fusion.1), channel_id=1, source_target_pairs={{0,32},{16,48},{32,64},{48,80},{64,96},{80,112},{96,0},{112,16},{1... | collective-permute-start | bytes 393224 | tf_op jit(solution)/shard_map/ppermute | solution.py:29
  171.8 27.7 %collective-permute-start.2 = (bf16[2,2,2,16,512]{4,3,2,1,0:T(8,128)(2,1)S(1)}, bf16[2,2,2,16,512]{4,3,2,1,0:T(8,128)(2,1)S(1)}, u32[]{:S(2)}, u32[]{:S(2)}) collective-permute-start(bf16[2,2,2,16,512]{4,3,2,1,0:T(8,128)(2,1)S(1)} %pad_maximum_fusion.1), channel_id=1, source_target_pairs={{0,48},{16,64},{32,80},{48,96},{64,112},{80,0},{96,16},{112,32},{1... | collective-permute-start | bytes 393224 | tf_op jit(solution)/shard_map/ppermute | solution.py:29
  175.4 24.1 %collective-permute-start.3 = (bf16[2,2,2,16,512]{4,3,2,1,0:T(8,128)(2,1)S(1)}, bf16[2,2,2,16,512]{4,3,2,1,0:T(8,128)(2,1)S(1)}, u32[]{:S(2)}, u32[]{:S(2)}) collective-permute-start(bf16[2,2,2,16,512]{4,3,2,1,0:T(8,128)(2,1)S(1)} %pad_maximum_fusion.1), channel_id=1, source_target_pairs={{0,64},{16,80},{32,96},{48,112},{64,0},{80,16},{96,32},{112,48},{1... | collective-permute-start | bytes 393224 | tf_op jit(solution)/shard_map/ppermute | solution.py:29
  176.3 23.3 %collective-permute-start.4 = (bf16[2,2,2,16,512]{4,3,2,1,0:T(8,128)(2,1)S(1)}, bf16[2,2,2,16,512]{4,3,2,1,0:T(8,128)(2,1)S(1)}, u32[]{:S(2)}, u32[]{:S(2)}) collective-permute-start(bf16[2,2,2,16,512]{4,3,2,1,0:T(8,128)(2,1)S(1)} %pad_maximum_fusion.1), channel_id=1, source_target_pairs={{0,80},{16,96},{32,112},{48,0},{64,16},{80,32},{96,48},{112,64},{1... | collective-permute-start | bytes 393224 | tf_op jit(solution)/shard_map/ppermute | solution.py:29
  194.5 11.6 %collective-permute-start.6 = (bf16[2,2,2,16,512]{4,3,2,1,0:T(8,128)(2,1)S(1)}, bf16[2,2,2,16,512]{4,3,2,1,0:T(8,128)(2,1)S(1)}, u32[]{:S(2)}, u32[]{:S(2)}) collective-permute-start(bf16[2,2,2,16,512]{4,3,2,1,0:T(8,128)(2,1)S(1)} %pad_maximum_fusion.1), channel_id=1, source_target_pairs={{0,112},{16,0},{32,16},{48,32},{64,48},{80,64},{96,80},{112,96},{1... | collective-permute-start | bytes 393224 | tf_op jit(solution)/shard_map/ppermute | solution.py:29
  217.4 14.7 %collective-permute-start.29 = (bf16[2,16,16,64]{3,2,1,0:T(8,128)(2,1)S(1)}, bf16[2,16,16,64]{3,2,1,0:T(8,128)(2,1)S(1)}, u32[]{:S(2)}, u32[]{:S(2)}) collective-permute-start(bf16[2,16,16,64]{3,2,1,0:T(8,128)(2,1)S(1)} %get-tuple-element.30), channel_id=1, source_target_pairs={{0,16},{16,32},{32,48},{48,64},{64,80},{80,96},{96,112},{112,0},{1... | collective-permute-start | bytes 196616 | tf_op jit(solution)/shard_map/ppermute | solution.py:29
  219.8 12.9 %collective-permute-start.30 = (bf16[2,16,16,64]{3,2,1,0:T(8,128)(2,1)S(1)}, bf16[2,16,16,64]{3,2,1,0:T(8,128)(2,1)S(1)}, u32[]{:S(2)}, u32[]{:S(2)}) collective-permute-start(bf16[2,16,16,64]{3,2,1,0:T(8,128)(2,1)S(1)} %get-tuple-element.30), channel_id=1, source_target_pairs={{0,32},{16,48},{32,64},{48,80},{64,96},{80,112},{96,0},{112,16},{1... | collective-permute-start | bytes 196616 | tf_op jit(solution)/shard_map/ppermute | solution.py:29
  220.1 16.9 %collective-permute-start.31 = (bf16[2,16,16,64]{3,2,1,0:T(8,128)(2,1)S(1)}, bf16[2,16,16,64]{3,2,1,0:T(8,128)(2,1)S(1)}, u32[]{:S(2)}, u32[]{:S(2)}) collective-permute-start(bf16[2,16,16,64]{3,2,1,0:T(8,128)(2,1)S(1)} %get-tuple-element.30), channel_id=1, source_target_pairs={{0,48},{16,64},{32,80},{48,96},{64,112},{80,0},{96,16},{112,32},{1... | collective-permute-start | bytes 196616 | tf_op jit(solution)/shard_map/ppermute | solution.py:29
  227.0 10.0 %collective-permute-start.32 = (bf16[2,16,16,64]{3,2,1,0:T(8,128)(2,1)S(1)}, bf16[2,16,16,64]{3,2,1,0:T(8,128)(2,1)S(1)}, u32[]{:S(2)}, u32[]{:S(2)}) collective-permute-start(bf16[2,16,16,64]{3,2,1,0:T(8,128)(2,1)S(1)} %get-tuple-element.30), channel_id=1, source_target_pairs={{0,64},{16,80},{32,96},{48,112},{64,0},{80,16},{96,32},{112,48},{1... | collective-permute-start | bytes 196616 | tf_op jit(solution)/shard_map/ppermute | solution.py:29
  227.9 11.4 %collective-permute-start.33 = (bf16[2,16,16,64]{3,2,1,0:T(8,128)(2,1)S(1)}, bf16[2,16,16,64]{3,2,1,0:T(8,128)(2,1)S(1)}, u32[]{:S(2)}, u32[]{:S(2)}) collective-permute-start(bf16[2,16,16,64]{3,2,1,0:T(8,128)(2,1)S(1)} %get-tuple-element.30), channel_id=1, source_target_pairs={{0,80},{16,96},{32,112},{48,0},{64,16},{80,32},{96,48},{112,64},{1... | collective-permute-start | bytes 196616 | tf_op jit(solution)/shard_map/ppermute | solution.py:29
  260.6 25.5 %collective-permute-start.66 = (f32[2,2,64]{2,1,0:T(2,128)S(1)}, f32[2,2,64]{2,1,0:T(2,128)}, u32[]{:S(2)}, u32[]{:S(2)}) collective-permute-start(f32[2,2,64]{2,1,0:T(2,128)S(1)} %pad_maximum_fusion.2), channel_id=1, source_target_pairs={{0,16},{16,32},{32,48},{48,64},{64,80},{80,96},{96,112},{112,0},{1... | collective-permute-start | bytes 3080 | tf_op jit(solution)/shard_map/ppermute | solution.py:29
  264.6 24.5 %collective-permute-start.67 = (f32[2,2,64]{2,1,0:T(2,128)S(1)}, f32[2,2,64]{2,1,0:T(2,128)}, u32[]{:S(2)}, u32[]{:S(2)}) collective-permute-start(f32[2,2,64]{2,1,0:T(2,128)S(1)} %pad_maximum_fusion.2), channel_id=1, source_target_pairs={{0,32},{16,48},{32,64},{48,80},{64,96},{80,112},{96,0},{112,16},{1... | collective-permute-start | bytes 3080 | tf_op jit(solution)/shard_map/ppermute | solution.py:29
  265.3 28.8 %collective-permute-start.68 = (f32[2,2,64]{2,1,0:T(2,128)S(1)}, f32[2,2,64]{2,1,0:T(2,128)S(1)}, u32[]{:S(2)}, u32[]{:S(2)}) collective-permute-start(f32[2,2,64]{2,1,0:T(2,128)S(1)} %pad_maximum_fusion.2), channel_id=1, source_target_pairs={{0,48},{16,64},{32,80},{48,96},{64,112},{80,0},{96,16},{112,32},{1... | collective-permute-start | bytes 3080 | tf_op jit(solution)/shard_map/ppermute | solution.py:29
  269.0 28.8 %collective-permute-start.69 = (f32[2,2,64]{2,1,0:T(2,128)S(1)}, f32[2,2,64]{2,1,0:T(2,128)S(1)}, u32[]{:S(2)}, u32[]{:S(2)}) collective-permute-start(f32[2,2,64]{2,1,0:T(2,128)S(1)} %pad_maximum_fusion.2), channel_id=1, source_target_pairs={{0,64},{16,80},{32,96},{48,112},{64,0},{80,16},{96,32},{112,48},{1... | collective-permute-start | bytes 3080 | tf_op jit(solution)/shard_map/ppermute | solution.py:29
  271.4 27.3 %collective-permute-start.70 = (f32[2,2,64]{2,1,0:T(2,128)S(1)}, f32[2,2,64]{2,1,0:T(2,128)S(1)}, u32[]{:S(2)}, u32[]{:S(2)}) collective-permute-start(f32[2,2,64]{2,1,0:T(2,128)S(1)} %pad_maximum_fusion.2), channel_id=1, source_target_pairs={{0,80},{16,96},{32,112},{48,0},{64,16},{80,32},{96,48},{112,64},{1... | collective-permute-start | bytes 3080 | tf_op jit(solution)/shard_map/ppermute | solution.py:29
  286.1 18.2 %collective-permute-start.71 = (f32[2,2,64]{2,1,0:T(2,128)S(1)}, f32[2,2,64]{2,1,0:T(2,128)S(1)}, u32[]{:S(2)}, u32[]{:S(2)}) collective-permute-start(f32[2,2,64]{2,1,0:T(2,128)S(1)} %pad_maximum_fusion.2), channel_id=1, source_target_pairs={{0,96},{16,112},{32,0},{48,16},{64,32},{80,48},{96,64},{112,80},{1... | collective-permute-start | bytes 3080 | tf_op jit(solution)/shard_map/ppermute | solution.py:29
  289.1 16.5 %collective-permute-start.72 = (f32[2,2,64]{2,1,0:T(2,128)S(1)}, f32[2,2,64]{2,1,0:T(2,128)S(1)}, u32[]{:S(2)}, u32[]{:S(2)}) collective-permute-start(f32[2,2,64]{2,1,0:T(2,128)S(1)} %pad_maximum_fusion.2), channel_id=1, source_target_pairs={{0,112},{16,0},{32,16},{48,32},{64,48},{80,64},{96,80},{112,96},{1... | collective-permute-start | bytes 3080 | tf_op jit(solution)/shard_map/ppermute | solution.py:29
  294.1 18.5 %collective-permute-start.37 = (bf16[2,2,16,64]{3,2,1,0:T(8,128)(2,1)}, bf16[2,2,16,64]{3,2,1,0:T(8,128)(2,1)}, u32[]{:S(2)}, u32[]{:S(2)}) collective-permute-start(bf16[2,2,16,64]{3,2,1,0:T(8,128)(2,1)} %get-tuple-element.74), channel_id=1, source_target_pairs={{0,16},{16,32},{32,48},{48,64},{64,80},{80,96},{96,112},{112,0},{1... | collective-permute-start | bytes 24584 | tf_op jit(solution)/shard_map/ppermute | solution.py:49
  297.8 18.1 %collective-permute-start.38 = (bf16[2,2,16,64]{3,2,1,0:T(8,128)(2,1)}, bf16[2,2,16,64]{3,2,1,0:T(8,128)(2,1)}, u32[]{:S(2)}, u32[]{:S(2)}) collective-permute-start(bf16[2,2,16,64]{3,2,1,0:T(8,128)(2,1)} %get-tuple-element.73), channel_id=1, source_target_pairs={{0,32},{16,48},{32,64},{48,80},{64,96},{80,112},{96,0},{112,16},{1... | collective-permute-start | bytes 24584 | tf_op jit(solution)/shard_map/ppermute | solution.py:49
  298.7 21.4 %collective-permute-start.39 = (bf16[2,2,16,64]{3,2,1,0:T(8,128)(2,1)}, bf16[2,2,16,64]{3,2,1,0:T(8,128)(2,1)}, u32[]{:S(2)}, u32[]{:S(2)}) collective-permute-start(bf16[2,2,16,64]{3,2,1,0:T(8,128)(2,1)} %get-tuple-element.72), channel_id=1, source_target_pairs={{0,48},{16,64},{32,80},{48,96},{64,112},{80,0},{96,16},{112,32},{1... | collective-permute-start | bytes 24584 | tf_op jit(solution)/shard_map/ppermute | solution.py:49
  304.3 28.3 %collective-permute-start.40 = (bf16[2,2,16,64]{3,2,1,0:T(8,128)(2,1)}, bf16[2,2,16,64]{3,2,1,0:T(8,128)(2,1)}, u32[]{:S(2)}, u32[]{:S(2)}) collective-permute-start(bf16[2,2,16,64]{3,2,1,0:T(8,128)(2,1)} %get-tuple-element.71), channel_id=1, source_target_pairs={{0,64},{16,80},{32,96},{48,112},{64,0},{80,16},{96,32},{112,48},{1... | collective-permute-start | bytes 24584 | tf_op jit(solution)/shard_map/ppermute | solution.py:49
  305.6 28.3 %collective-permute-start.41 = (bf16[2,2,16,64]{3,2,1,0:T(8,128)(2,1)}, bf16[2,2,16,64]{3,2,1,0:T(8,128)(2,1)}, u32[]{:S(2)}, u32[]{:S(2)}) collective-permute-start(bf16[2,2,16,64]{3,2,1,0:T(8,128)(2,1)} %get-tuple-element.70), channel_id=1, source_target_pairs={{0,80},{16,96},{32,112},{48,0},{64,16},{80,32},{96,48},{112,64},{1... | collective-permute-start | bytes 24584 | tf_op jit(solution)/shard_map/ppermute | solution.py:49
  312.6 21.4 %collective-permute-start.42 = (bf16[2,2,16,64]{3,2,1,0:T(8,128)(2,1)}, bf16[2,2,16,64]{3,2,1,0:T(8,128)(2,1)S(1)}, u32[]{:S(2)}, u32[]{:S(2)}) collective-permute-start(bf16[2,2,16,64]{3,2,1,0:T(8,128)(2,1)} %get-tuple-element.69), channel_id=1, source_target_pairs={{0,96},{16,112},{32,0},{48,16},{64,32},{80,48},{96,64},{112,80},{1... | collective-permute-start | bytes 24584 | tf_op jit(solution)/shard_map/ppermute | solution.py:49
  315.9 18.2 %collective-permute-start.43 = (bf16[2,2,16,64]{3,2,1,0:T(8,128)(2,1)}, bf16[2,2,16,64]{3,2,1,0:T(8,128)(2,1)S(1)}, u32[]{:S(2)}, u32[]{:S(2)}) collective-permute-start(bf16[2,2,16,64]{3,2,1,0:T(8,128)(2,1)} %get-tuple-element.68), channel_id=1, source_target_pairs={{0,112},{16,0},{32,16},{48,32},{64,48},{80,64},{96,80},{112,96},{1... | collective-permute-start | bytes 24584 | tf_op jit(solution)/shard_map/ppermute | solution.py:49
  320.1 17.4 %collective-permute-start.58 = (bf16[32,27,64]{2,0,1:T(8,128)(2,1)}, bf16[32,27,64]{2,0,1:T(8,128)(2,1)}, u32[]{:S(2)}, u32[]{:S(2)}) collective-permute-start(bf16[32,27,64]{2,0,1:T(8,128)(2,1)} %get-tuple-element.36), channel_id=1, source_target_pairs={{0,15},{1,0},{2,1},{3,2},{4,3},{5,4},{6,5},{7,6},{8,7},{9,8},{10,9... | collective-permute-start | bytes 331784 | tf_op jit(solution)/shard_map/ppermute | solution.py:64
  332.6 10.1 %collective-permute-start.57 = (bf16[32,27,64]{2,0,1:T(8,128)(2,1)}, bf16[32,27,64]{2,0,1:T(8,128)(2,1)}, u32[]{:S(2)}, u32[]{:S(2)}) collective-permute-start(bf16[32,27,64]{2,0,1:T(8,128)(2,1)} %get-tuple-element.37), channel_id=1, source_target_pairs={{0,14},{1,15},{2,0},{3,1},{4,2},{5,3},{6,4},{7,5},{8,6},{9,7},{10,... | collective-permute-start | bytes 331784 | tf_op jit(solution)/shard_map/ppermute | solution.py:64
  334.0 13.0 %collective-permute-start.56 = (bf16[32,27,64]{2,0,1:T(8,128)(2,1)}, bf16[32,27,64]{2,0,1:T(8,128)(2,1)}, u32[]{:S(2)}, u32[]{:S(2)}) collective-permute-start(bf16[32,27,64]{2,0,1:T(8,128)(2,1)} %get-tuple-element.38), channel_id=1, source_target_pairs={{0,13},{1,14},{2,15},{3,0},{4,1},{5,2},{6,3},{7,4},{8,5},{9,6},{10... | collective-permute-start | bytes 331784 | tf_op jit(solution)/shard_map/ppermute | solution.py:64
  334.0 37.6 %collective-permute-start.55 = (bf16[32,27,64]{2,0,1:T(8,128)(2,1)}, bf16[32,27,64]{2,0,1:T(8,128)(2,1)}, u32[]{:S(2)}, u32[]{:S(2)}) collective-permute-start(bf16[32,27,64]{2,0,1:T(8,128)(2,1)} %get-tuple-element.39), channel_id=1, source_target_pairs={{0,12},{1,13},{2,14},{3,15},{4,0},{5,1},{6,2},{7,3},{8,4},{9,5},{1... | collective-permute-start | bytes 331784 | tf_op jit(solution)/shard_map/ppermute | solution.py:64
  334.1 37.5 %collective-permute-start.54 = (bf16[32,27,64]{2,0,1:T(8,128)(2,1)}, bf16[32,27,64]{2,0,1:T(8,128)(2,1)}, u32[]{:S(2)}, u32[]{:S(2)}) collective-permute-start(bf16[32,27,64]{2,0,1:T(8,128)(2,1)} %get-tuple-element.40), channel_id=1, source_target_pairs={{0,11},{1,12},{2,13},{3,14},{4,15},{5,0},{6,1},{7,2},{8,3},{9,4},{... | collective-permute-start | bytes 331784 | tf_op jit(solution)/shard_map/ppermute | solution.py:64
  337.5 41.8 %collective-permute-start.53 = (bf16[32,27,64]{2,0,1:T(8,128)(2,1)}, bf16[32,27,64]{2,0,1:T(8,128)(2,1)}, u32[]{:S(2)}, u32[]{:S(2)}) collective-permute-start(bf16[32,27,64]{2,0,1:T(8,128)(2,1)} %get-tuple-element.41), channel_id=1, source_target_pairs={{0,10},{1,11},{2,12},{3,13},{4,14},{5,15},{6,0},{7,1},{8,2},{9,3},... | collective-permute-start | bytes 331784 | tf_op jit(solution)/shard_map/ppermute | solution.py:64
  342.7 36.6 %collective-permute-start.52 = (bf16[32,27,64]{2,0,1:T(8,128)(2,1)}, bf16[32,27,64]{2,0,1:T(8,128)(2,1)}, u32[]{:S(2)}, u32[]{:S(2)}) collective-permute-start(bf16[32,27,64]{2,0,1:T(8,128)(2,1)} %get-tuple-element.42), channel_id=1, source_target_pairs={{0,9},{1,10},{2,11},{3,12},{4,13},{5,14},{6,15},{7,0},{8,1},{9,2},... | collective-permute-start | bytes 331784 | tf_op jit(solution)/shard_map/ppermute | solution.py:64
  347.0 54.5 %collective-permute-start.51 = (bf16[32,27,64]{2,0,1:T(8,128)(2,1)}, bf16[32,27,64]{2,0,1:T(8,128)(2,1)}, u32[]{:S(2)}, u32[]{:S(2)}) collective-permute-start(bf16[32,27,64]{2,0,1:T(8,128)(2,1)} %get-tuple-element.43), channel_id=1, source_target_pairs={{0,8},{1,9},{2,10},{3,11},{4,12},{5,13},{6,14},{7,15},{8,0},{9,1},... | collective-permute-start | bytes 331784 | tf_op jit(solution)/shard_map/ppermute | solution.py:64
  371.6 30.1 %collective-permute-start.50 = (bf16[32,27,64]{2,0,1:T(8,128)(2,1)}, bf16[32,27,64]{2,0,1:T(8,128)(2,1)}, u32[]{:S(2)}, u32[]{:S(2)}) collective-permute-start(bf16[32,27,64]{2,0,1:T(8,128)(2,1)} %get-tuple-element.44), channel_id=1, source_target_pairs={{0,7},{1,8},{2,9},{3,10},{4,11},{5,12},{6,13},{7,14},{8,15},{9,0},... | collective-permute-start | bytes 331784 | tf_op jit(solution)/shard_map/ppermute | solution.py:64
  371.6 30.2 %collective-permute-start.49 = (bf16[32,27,64]{2,0,1:T(8,128)(2,1)}, bf16[32,27,64]{2,0,1:T(8,128)(2,1)}, u32[]{:S(2)}, u32[]{:S(2)}) collective-permute-start(bf16[32,27,64]{2,0,1:T(8,128)(2,1)} %get-tuple-element.45), channel_id=1, source_target_pairs={{0,6},{1,7},{2,8},{3,9},{4,10},{5,11},{6,12},{7,13},{8,14},{9,15},... | collective-permute-start | bytes 331784 | tf_op jit(solution)/shard_map/ppermute | solution.py:64
  379.3 37.3 %collective-permute-start.48 = (bf16[32,27,64]{2,0,1:T(8,128)(2,1)}, bf16[32,27,64]{2,0,1:T(8,128)(2,1)}, u32[]{:S(2)}, u32[]{:S(2)}) collective-permute-start(bf16[32,27,64]{2,0,1:T(8,128)(2,1)} %get-tuple-element.46), channel_id=1, source_target_pairs={{0,5},{1,6},{2,7},{3,8},{4,9},{5,10},{6,11},{7,12},{8,13},{9,14},{... | collective-permute-start | bytes 331784 | tf_op jit(solution)/shard_map/ppermute | solution.py:64
  379.3 37.3 %collective-permute-start.47 = (bf16[32,27,64]{2,0,1:T(8,128)(2,1)}, bf16[32,27,64]{2,0,1:T(8,128)(2,1)}, u32[]{:S(2)}, u32[]{:S(2)}) collective-permute-start(bf16[32,27,64]{2,0,1:T(8,128)(2,1)} %get-tuple-element.47), channel_id=1, source_target_pairs={{0,4},{1,5},{2,6},{3,7},{4,8},{5,9},{6,10},{7,11},{8,12},{9,13},{1... | collective-permute-start | bytes 331784 | tf_op jit(solution)/shard_map/ppermute | solution.py:64
  401.5 15.1 %collective-permute-start.46 = (bf16[32,27,64]{2,0,1:T(8,128)(2,1)}, bf16[32,27,64]{2,0,1:T(8,128)(2,1)}, u32[]{:S(2)}, u32[]{:S(2)}) collective-permute-start(bf16[32,27,64]{2,0,1:T(8,128)(2,1)} %get-tuple-element.48), channel_id=1, source_target_pairs={{0,3},{1,4},{2,5},{3,6},{4,7},{5,8},{6,9},{7,10},{8,11},{9,12},{10... | collective-permute-start | bytes 331784 | tf_op jit(solution)/shard_map/ppermute | solution.py:64
  401.7 14.9 %collective-permute-start.45 = (bf16[32,27,64]{2,0,1:T(8,128)(2,1)}, bf16[32,27,64]{2,0,1:T(8,128)(2,1)}, u32[]{:S(2)}, u32[]{:S(2)}) collective-permute-start(bf16[32,27,64]{2,0,1:T(8,128)(2,1)} %get-tuple-element.49), channel_id=1, source_target_pairs={{0,2},{1,3},{2,4},{3,5},{4,6},{5,7},{6,8},{7,9},{8,10},{9,11},{10,... | collective-permute-start | bytes 331784 | tf_op jit(solution)/shard_map/ppermute | solution.py:64
  401.8 14.8 %collective-permute-start.44 = (bf16[32,27,64]{2,0,1:T(8,128)(2,1)}, bf16[32,27,64]{2,0,1:T(8,128)(2,1)}, u32[]{:S(2)}, u32[]{:S(2)}) collective-permute-start(bf16[32,27,64]{2,0,1:T(8,128)(2,1)} %get-tuple-element.35), channel_id=1, source_target_pairs={{0,1},{1,2},{2,3},{3,4},{4,5},{5,6},{6,7},{7,8},{8,9},{9,10},{10,1... | collective-permute-start | bytes 331784 | tf_op jit(solution)/shard_map/ppermute | solution.py:64
  420.0 16.1 %collective-permute-start.59 = (f32[32,27,64]{2,0,1:T(8,128)}, f32[32,27,64]{2,0,1:T(8,128)S(1)}, u32[]{:S(2)}, u32[]{:S(2)}) collective-permute-start(f32[32,27,64]{2,0,1:T(8,128)} %get-tuple-element.26), channel_id=1, source_target_pairs={{0,16},{16,32},{32,48},{48,64},{64,80},{80,96},{96,112},{112,0},{1... | collective-permute-start | bytes 663560 | tf_op jit(solution)/shard_map/ppermute | solution.py:29
  423.4 31.0 %collective-permute-start.60 = (f32[32,27,64]{2,0,1:T(8,128)}, f32[32,27,64]{2,0,1:T(8,128)S(1)}, u32[]{:S(2)}, u32[]{:S(2)}) collective-permute-start(f32[32,27,64]{2,0,1:T(8,128)} %get-tuple-element.26), channel_id=1, source_target_pairs={{0,32},{16,48},{32,64},{48,80},{64,96},{80,112},{96,0},{112,16},{1... | collective-permute-start | bytes 663560 | tf_op jit(solution)/shard_map/ppermute | solution.py:29
  423.4 31.8 %collective-permute-start.61 = (f32[32,27,64]{2,0,1:T(8,128)}, f32[32,27,64]{2,0,1:T(8,128)S(1)}, u32[]{:S(2)}, u32[]{:S(2)}) collective-permute-start(f32[32,27,64]{2,0,1:T(8,128)} %get-tuple-element.26), channel_id=1, source_target_pairs={{0,48},{16,64},{32,80},{48,96},{64,112},{80,0},{96,16},{112,32},{1... | collective-permute-start | bytes 663560 | tf_op jit(solution)/shard_map/ppermute | solution.py:29
  431.2 24.8 %collective-permute-start.62 = (f32[32,27,64]{2,0,1:T(8,128)}, f32[32,27,64]{2,0,1:T(8,128)S(1)}, u32[]{:S(2)}, u32[]{:S(2)}) collective-permute-start(f32[32,27,64]{2,0,1:T(8,128)} %get-tuple-element.26), channel_id=1, source_target_pairs={{0,64},{16,80},{32,96},{48,112},{64,0},{80,16},{96,32},{112,48},{1... | collective-permute-start | bytes 663560 | tf_op jit(solution)/shard_map/ppermute | solution.py:29
  432.2 32.8 %collective-permute-start.63 = (f32[32,27,64]{2,0,1:T(8,128)}, f32[32,27,64]{2,0,1:T(8,128)S(1)}, u32[]{:S(2)}, u32[]{:S(2)}) collective-permute-start(f32[32,27,64]{2,0,1:T(8,128)} %get-tuple-element.26), channel_id=1, source_target_pairs={{0,80},{16,96},{32,112},{48,0},{64,16},{80,32},{96,48},{112,64},{1... | collective-permute-start | bytes 663560 | tf_op jit(solution)/shard_map/ppermute | solution.py:29
  436.2 29.6 %collective-permute-start.64 = (f32[32,27,64]{2,0,1:T(8,128)}, f32[32,27,64]{2,0,1:T(8,128)S(1)}, u32[]{:S(2)}, u32[]{:S(2)}) collective-permute-start(f32[32,27,64]{2,0,1:T(8,128)} %get-tuple-element.26), channel_id=1, source_target_pairs={{0,96},{16,112},{32,0},{48,16},{64,32},{80,48},{96,64},{112,80},{1... | collective-permute-start | bytes 663560 | tf_op jit(solution)/shard_map/ppermute | solution.py:29
  454.4 53.0 %collective-permute-start.65 = (f32[32,27,64]{2,0,1:T(8,128)}, f32[32,27,64]{2,0,1:T(8,128)S(1)}, u32[]{:S(2)}, u32[]{:S(2)}) collective-permute-start(f32[32,27,64]{2,0,1:T(8,128)} %get-tuple-element.26), channel_id=1, source_target_pairs={{0,112},{16,0},{32,16},{48,32},{64,48},{80,64},{96,80},{112,96},{1... | collective-permute-start | bytes 663560 | tf_op jit(solution)/shard_map/ppermute | solution.py:29
  (29 other events, 843.4 us)
